TPU v7x, 256 devices: a whole 4x4x8 slice. The times are simulated.
256 devices in a mesh: tm: 32 (over z, x), region: 8 (over y, core).
Axes of the slice: x: 4, y: 4, z: 8, core: 2. Of those that a mesh axis runs over, the one named last changes fastest.
Arguments:
- start_primal: float32 [2048, 8, 3200], P('tm', 'region'), may hold values from 0 to 10, as said below
- demand: float32 [2048, 8, 3200], P('tm', 'region'), may hold values from -30 to 30
- unit_cost: float32 [8, 3200], P('region'), may hold values from -5 to 5
- build_cost: float32 [8, 128], P('region', 'tm'), may hold values from 0.5 to 2
- start_capacity: float32 [8, 128], P('region', 'tm'), may hold values from 0 to 2
- net_weights: float32 [8, 25, 3, 128, 128], P('region'), may hold values from -0.3125 to 0.3125
- net_columns: int32 [8, 25, 3], P('region'), may hold values from 0 to 24
- line_weights: float32 [8, 4, 128, 128], P('region'), may hold values from -0.25 to 0.25
- line_source: int32 [8, 4], replicated, may hold values from 0 to 7
- generator_map: int32 [8, 128], P('region'), may hold values from 0 to 127
Outputs:
- primal_final: float32 [2048, 8, 3200], P('tm', 'region')
- dual_final: float32 [2048, 8, 3200], P('tm', 'region')
- capacity_final: float32 [8, 128], P('region', 'tm')
Inputs may be any that keep to these rules, and one draw needn't show every extreme that they name: `start_primal`: Nonnegative.
All inputs are finite; a program needn't handle non-finite values.
Results may differ from a plain program's by a relative error of at most 0.0003.
Values sent between devices are 32-bit elements; how exact they have to be, the bound alone decides.
A program may use at most 64 MiB of HBM per device.

v0:
```python
import math

import jax
import jax.numpy as jnp
from jax import lax
from jax.sharding import PartitionSpec as P

ITERS = 4


HIGHEST_PRECISION = lax.Precision.HIGHEST
STEP_SCALE = 0.2
EPSILON = 1e-06


def shifted(shard, axis, by):
    devices = lax.axis_size(axis)
    pairs = [(i, i + by) for i in range(devices) if 0 <= i + by < devices]
    return lax.ppermute(shard, axis, pairs)


def network_forward(blocks, weights, columns):
    hour_count = blocks.shape[0]
    picked = jnp.take(blocks, columns.reshape(-1), axis=1)
    flat_weights = weights.reshape(-1, weights.shape[2], weights.shape[3])
    product = jnp.einsum("hpk,pkl->hpl", picked, flat_weights, precision=HIGHEST_PRECISION)
    return product.reshape(hour_count, columns.shape[0], columns.shape[1], -1).sum(axis=2)


def network_adjoint(dual_rows, weights, columns):
    hour_count = dual_rows.shape[0]
    partial_value = jnp.einsum("hil,iskl->hisk", dual_rows, weights, precision=HIGHEST_PRECISION)
    block_count = columns.shape[0]
    placing = (columns.reshape(-1)[:, None] == jnp.arange(block_count)[None, :]).astype(jnp.float32)
    stacked = partial_value.reshape(hour_count, -1, partial_value.shape[3])
    return jnp.einsum("hpk,pc->hck", stacked, placing, precision=HIGHEST_PRECISION)


def body(
    start_primal,
    demand,
    unit_cost,
    build_cost,
    start_capacity,
    net_weights,
    net_columns,
    line_weights,
    line_source,
    generator_map,
):
    hour_count, _, row_width = start_primal.shape
    block_size = net_weights.shape[3]
    block_count = row_width // block_size
    tm_count = lax.axis_size("tm")
    region_count = lax.axis_size("region")
    own_region = lax.axis_index("region")
    weights = net_weights[0]
    columns = net_columns[0]
    line_mats = line_weights[0]
    unit_rows = unit_cost.reshape(block_count, block_size)
    invest_own = start_capacity.shape[1]
    invest_all = invest_own * tm_count
    couple = 1.0 / math.sqrt(hour_count * tm_count)
    primal_count = hour_count * tm_count * region_count * row_width + region_count * invest_all
    dual_count = hour_count * tm_count * region_count * row_width
    selector = (generator_map[0][:, None] == jnp.arange(invest_all)[None, :]).astype(jnp.float32)
    line_links = (line_source[:, :, None] == jnp.arange(region_count)[None, None, :]).astype(
        jnp.float32
    )
    own_sources = lax.dynamic_index_in_dim(line_links, own_region, 0, keepdims=False)
    free_column = (jnp.arange(block_count) == 3)[None, :, None]
    free_row = (jnp.arange(block_count) < 3)[None, :, None]
    primal = start_primal.reshape(hour_count, block_count, block_size)
    target = demand.reshape(hour_count, block_count, block_size)
    dual = jnp.zeros_like(primal)
    primal_weight = jnp.float32(1.0)
    capacity, build_rows = (
        lax.all_gather(start_capacity[0], "tm", axis=0, tiled=True),
        lax.all_gather(build_cost[0], "tm", axis=0, tiled=True),
    )
    for iteration in range(ITERS):
        primal_step = STEP_SCALE / primal_weight
        dual_step = STEP_SCALE * primal_weight
        adjoint = network_adjoint(dual, weights, columns)
        after = shifted(dual[0, 0], "tm", -1)
        following = jnp.concatenate([dual[1:, 0], after[None]], axis=0)
        partial_lines = jnp.einsum(
            "hl,jkl->jhk", dual[:, 1], line_mats, precision=HIGHEST_PRECISION
        )
        line_back = lax.psum_scatter(
            jnp.einsum("jq,jhk->qhk", own_sources, partial_lines, precision=HIGHEST_PRECISION),
            "region",
            scatter_dimension=0,
            tiled=True,
        )[0]
        adjoint = adjoint.at[:, 0].add(-following).at[:, 3].add(line_back)
        column_sums = jnp.sum(dual[:, 2], axis=0)
        capacity_part = couple * jnp.dot(column_sums, selector, precision=HIGHEST_PRECISION)
        moved = primal - primal_step * (unit_rows[None] - adjoint)
        new_primal = jnp.where(free_column, moved, jnp.maximum(moved, 0.0))
        capacity_grad = lax.psum(capacity_part, "tm")
        new_capacity = jnp.maximum(capacity - primal_step * (build_rows - capacity_grad), 0.0)
        capacity_bar = 2.0 * new_capacity - capacity
        capacity_change = lax.dynamic_slice_in_dim(
            new_capacity - capacity, lax.axis_index("tm") * invest_own, invest_own, 0
        )
        primal_bar = 2.0 * new_primal - primal
        primal_local = jnp.sum((new_primal - primal) ** 2) + jnp.sum(capacity_change**2)
        if iteration + 1 < ITERS:
            primal_total = lax.psum(primal_local, ("tm", "region"))
        applied = network_forward(primal_bar, weights, columns)
        before = shifted(primal_bar[-1, 0], "tm", 1)
        earlier = jnp.concatenate([before[None], primal_bar[:-1, 0]], axis=0)
        chosen_flows = jnp.einsum(
            "jr,rhk->jhk",
            own_sources,
            lax.all_gather(primal_bar[:, 3][None], "region", axis=0, tiled=True),
            precision=HIGHEST_PRECISION,
        )
        line_flow = jnp.einsum("jhk,jkl->hl", chosen_flows, line_mats, precision=HIGHEST_PRECISION)
        picked_capacity = jnp.dot(selector, capacity_bar, precision=HIGHEST_PRECISION)
        applied = (
            applied.at[:, 0]
            .add(-earlier)
            .at[:, 1]
            .add(line_flow)
            .at[:, 2]
            .add(couple * picked_capacity[None])
        )
        moved_dual = dual + dual_step * (target - applied)
        new_dual = jnp.where(free_row, moved_dual, jnp.maximum(moved_dual, 0.0))
        if iteration + 1 < ITERS:
            dual_local = jnp.sum((new_dual - dual) ** 2)
            dual_total = lax.psum(dual_local, ("tm", "region"))
            primal_weight = jnp.sqrt(
                primal_weight
                * jnp.sqrt(primal_total / primal_count + EPSILON)
                / jnp.sqrt(dual_total / dual_count + EPSILON)
            )
        primal, dual, capacity = (new_primal, new_dual, new_capacity)
    capacity_own = lax.dynamic_slice_in_dim(
        capacity, lax.axis_index("tm") * invest_own, invest_own, 0
    )
    return (
        primal.reshape(hour_count, 1, row_width),
        dual.reshape(hour_count, 1, row_width),
        capacity_own[None],
    )


def solution(mesh):
    in_specs = (
        P("tm", "region", None),
        P("tm", "region", None),
        P("region", None),
        P("region", "tm"),
        P("region", "tm"),
        P("region", None, None, None, None),
        P("region", None, None),
        P("region", None, None, None),
        P(),
        P("region", None),
    )
    out_specs = (P("tm", "region", None), P("tm", "region", None), P("region", "tm"))
    return jax.shard_map(body, mesh=mesh, in_specs=in_specs, out_specs=out_specs, check_vma=False)
```

profile of v0, /device:TPU:1, one launch (start us, length us, event | category | flops | bytes accessed | tf_op | source)
XLA Modules:
  0.0 858.2 jit_solution(13189949462657411320)
XLA Ops:
  7.2 1.4 collective-permute-start
  9.4 1.3 convolution_bitcast_fusion.3
  12.1 0.8 copy.145
  12.9 9.0 %fusion.6 = f32[25,64,3,128]{3,1,2,0:T(8,128)S(1)} fusion(f32[1,25,3,128,128]{4,3,2,1,0:T(8,128)} %param.57), kind=kOutput, calls=%fused_computation.10 | convolution fusion | flops 943718400 | bytes 7372800 | tf_op jit(solution)/shard_map/hil,iskl->hisk/dot_general | solution.py:32
  22.0 2.4 fusion.14
  27.1 76.9 %all-reduce.6 = (f32[128]{0:T(128)S(1)}, f32[128]{0:T(128)S(1)}, f32[128]{0:T(128)S(1)}) all-reduce(f32[128]{0:T(128)S(1)} %bitcast_dynamic-update-slice_fusion.1, f32[128]{0:T(128)S(1)} %bitcast_dynamic-update-slice_fusion, f32[128]{0:T(128)S(1)} %fusion.51), channel_id=2, replica_groups=mesh['tm'=32,'region'=8] {'tm'}, use_global_device_ids=true, to_apply=%add.1 | all-reduce | flops 384 | bytes 3072 | tf_op jit(solution)/shard_map/all_gather | solution.py:78
  104.3 1.9 reduce.45
  106.3 3.1 reduce.43
  110.1 0.8 fusion.111
  110.8 1.0 fusion.60
  112.0 1.3 collective-permute-start.1
  113.3 28.2 %all-gather.2 = f32[512,1,128]{2,1,0:T(1,128)S(1)} all-gather(f32[64,1,128]{2,1,0:T(1,128)S(1)} %bitcast.385), channel_id=4, replica_groups=mesh['tm'=32,'region'=8] {'region'}, dimensions={0}, use_global_device_ids=true | all-gather | bytes 294912 | tf_op jit(solution)/shard_map/all_gather | solution.py:117
  141.5 2.1 gather_fusion
  143.6 7.9 fusion.22
  153.2 2.0 reduce_sum.150
  155.6 1.0 multiply_reduce_fusion.4
  157.0 10.5 %fusion.4 = f32[25,64,3,128]{3,1,2,0:T(8,128)} fusion(f32[1,25,3,128,128]{4,3,2,1,0:T(8,128)} %param.57, f32[64,25,128]{2,0,1:T(8,128)S(1)} %get-tuple-element.281), kind=kOutput, calls=%fused_computation.8 | convolution fusion | flops 943718400 | bytes 8192000 | tf_op jit(solution)/shard_map/hil,iskl->hisk/dot_general | solution.py:32
  167.7 55.8 %psum.73 = f32[128]{0:T(128)S(1)} all-reduce(f32[128]{0:T(128)S(1)} %fusion.49), channel_id=1, replica_groups=mesh['tm'=32,'region'=8] {'tm'}, use_global_device_ids=true, to_apply=%region_11.13 | all-reduce | flops 128 | bytes 1024 | tf_op jit(solution)/shard_map/psum | solution.py:101
  223.5 89.7 %all-reduce.5 = (f32[]{:T(128)}, f32[]{:T(128)}) all-reduce(f32[]{:T(128)S(6)} %add.249, f32[]{:T(128)} %get-tuple-element.280), channel_id=1, replica_groups=mesh['tm'=32,'region'=8] {'tm','region'}, use_global_device_ids=true, to_apply=%region_4.5 | all-reduce | flops 2 | bytes 16 | tf_op jit(solution)/shard_map/psum | solution.py:110
  314.6 1.3 collective-permute-start.2
  317.6 4.0 fusion.12
  321.8 0.8 slice.573
  322.7 1.4 copy.252
  325.8 22.6 %reduce-scatter.7.cloned.1.call-done = f32[1,64,128]{2,1,0:T(8,128)} async-done(((f32[8,64,128]{2,1,0:T(8,128)}), f32[1,64,128]{2,1,0:T(8,128)}) %reduce-scatter.7.cloned.1.call-update) | async-done | bytes 32784 | tf_op jit(solution)/shard_map/reduce_scatter | solution.py:90
  348.4 1.4 fusion.106
  349.7 2.2 multiply_reduce_fusion.3
  352.8 2.1 gather_fusion.1
  354.9 2.8 collective-permute-start.3
  357.8 16.1 %all-gather.3 = f32[512,1,128]{2,1,0:T(1,128)S(1)} all-gather(f32[64,1,128]{2,1,0:T(1,128)S(1)} %bitcast.383), channel_id=5, replica_groups=mesh['tm'=32,'region'=8] {'region'}, dimensions={0}, use_global_device_ids=true | all-gather | bytes 294912 | tf_op jit(solution)/shard_map/all_gather | solution.py:117
  373.9 7.9 fusion.20
  383.4 2.0 reduce_sum.155
  385.7 1.1 multiply_reduce_fusion.2
  387.2 10.5 %fusion.2 = f32[25,64,3,128]{3,1,2,0:T(8,128)} fusion(f32[1,25,3,128,128]{4,3,2,1,0:T(8,128)} %param.57, f32[64,25,128]{2,0,1:T(8,128)S(1)} %get-tuple-element.275), kind=kOutput, calls=%fused_computation.6 | convolution fusion | flops 943718400 | bytes 8192000 | tf_op jit(solution)/shard_map/hil,iskl->hisk/dot_general | solution.py:32
  397.9 59.1 %psum.76 = f32[128]{0:T(128)S(1)} all-reduce(f32[128]{0:T(128)S(1)} %fusion.47), channel_id=1, replica_groups=mesh['tm'=32,'region'=8] {'tm'}, use_global_device_ids=true, to_apply=%region_20.22 | all-reduce | flops 128 | bytes 1024 | tf_op jit(solution)/shard_map/psum | solution.py:101
  457.0 86.0 %all-reduce.4 = (f32[]{:T(128)}, f32[]{:T(128)}) all-reduce(f32[]{:T(128)S(6)} %add.257, f32[]{:T(128)} %get-tuple-element.274), channel_id=1, replica_groups=mesh['tm'=32,'region'=8] {'tm','region'}, use_global_device_ids=true, to_apply=%region_13.15 | all-reduce | flops 2 | bytes 16 | tf_op jit(solution)/shard_map/psum | solution.py:110
  544.5 1.3 collective-permute-start.4
  547.2 4.0 fusion.10
  551.4 0.8 slice.585
  552.2 1.4 copy.251
  555.4 23.9 %reduce-scatter.9.cloned.1.call-done = f32[1,64,128]{2,1,0:T(8,128)} async-done(((f32[8,64,128]{2,1,0:T(8,128)}), f32[1,64,128]{2,1,0:T(8,128)}) %reduce-scatter.9.cloned.1.call-update) | async-done | bytes 32784 | tf_op jit(solution)/shard_map/reduce_scatter | solution.py:90
  579.3 1.4 fusion.101
  580.7 2.2 multiply_reduce_fusion.1
  582.9 2.1 gather_fusion.2
  585.1 2.8 collective-permute-start.5
  587.9 16.1 %all-gather.4 = f32[512,1,128]{2,1,0:T(1,128)S(1)} all-gather(f32[64,1,128]{2,1,0:T(1,128)S(1)} %bitcast.384), channel_id=6, replica_groups=mesh['tm'=32,'region'=8] {'region'}, dimensions={0}, use_global_device_ids=true | all-gather | bytes 294912 | tf_op jit(solution)/shard_map/all_gather | solution.py:117
  604.0 7.9 fusion.18
  613.6 2.0 reduce_sum.160
  615.9 2.2 multiply_reduce_fusion
  618.5 10.5 %fusion = f32[25,64,3,128]{3,1,2,0:T(8,128)} fusion(f32[1,25,3,128,128]{4,3,2,1,0:T(8,128)} %param.57, f32[64,25,128]{2,0,1:T(8,128)S(1)} %get-tuple-element.271), kind=kOutput, calls=%fused_computation.4 | convolution fusion | flops 943718400 | bytes 8192000 | tf_op jit(solution)/shard_map/hil,iskl->hisk/dot_general | solution.py:32
  629.2 59.1 %psum.79 = f32[128]{0:T(128)S(1)} all-reduce(f32[128]{0:T(128)S(1)} %fusion.45), channel_id=1, replica_groups=mesh['tm'=32,'region'=8] {'tm'}, use_global_device_ids=true, to_apply=%region_29.31 | all-reduce | flops 128 | bytes 1024 | tf_op jit(solution)/shard_map/psum | solution.py:101
  688.3 86.0 %all-reduce.3 = (f32[]{:T(128)}, f32[]{:T(128)}) all-reduce(f32[]{:T(128)S(6)} %add.266, f32[]{:T(128)} %get-tuple-element.270), channel_id=1, replica_groups=mesh['tm'=32,'region'=8] {'tm','region'}, use_global_device_ids=true, to_apply=%region_22.24 | all-reduce | flops 2 | bytes 16 | tf_op jit(solution)/shard_map/psum | solution.py:110
  775.8 1.5 collective-permute-start.6
  778.5 4.0 fusion.8
  784.1 1.4 copy.250
  786.6 24.2 %reduce-scatter.11.cloned.1.call-done = f32[1,64,128]{2,1,0:T(8,128)} async-done(((f32[8,64,128]{2,1,0:T(8,128)}), f32[1,64,128]{2,1,0:T(8,128)}) %reduce-scatter.11.cloned.1.call-update) | async-done | bytes 32784 | tf_op jit(solution)/shard_map/reduce_scatter | solution.py:90
  810.8 1.4 fusion.96
  812.2 2.7 multiply_subtract_fusion
  814.9 2.2 gather_fusion.3
  817.0 2.8 collective-permute-start.7
  819.9 16.1 %all-gather.5 = f32[512,1,128]{2,1,0:T(1,128)S(1)} all-gather(f32[64,1,128]{2,1,0:T(1,128)S(1)} %bitcast.382), channel_id=7, replica_groups=mesh['tm'=32,'region'=8] {'region'}, dimensions={0}, use_global_device_ids=true | all-gather | bytes 294912 | tf_op jit(solution)/shard_map/all_gather | solution.py:117
  836.0 8.0 fusion.16
  844.9 1.7 reshape.912
  846.6 2.0 reduce_sum.162
  849.6 1.7 reshape.913
  (142 shorter events, 22.9 us)
Async XLA Ops:
  7.2 97.1 %copy-start = (f32[64,1,3200]{2,1,0:T(1,128)S(1)}, f32[64,1,3200]{2,1,0:T(1,128)}, u32[]{:S(2)}) copy-start(f32[64,1,3200]{2,1,0:T(1,128)} %param.53) | copy-start | bytes 2457604
  7.2 102.9 %reduce-scatter.5.cloned.1.call-start = ((), (), s32[]{:S(2)}) async-start(), calls=%async_computation.4 | async-start | bytes 294912 | tf_op jit(solution)/shard_map/reduce_scatter | solution.py:90
  7.2 102.8 %collective-permute-start = (f32[128]{0:T(128)S(1)}, f32[128]{0:T(128)S(1)}, u32[]{:S(2)}, u32[]{:S(2)}) collective-permute-start(f32[128]{0:T(128)S(1)} %broadcast.305), channel_id=1, source_target_pairs={{8,0},{16,8},{24,16},{32,24},{40,32},{48,40},{56,48},{64,56},{72,6... | collective-permute-start | bytes 1544 | tf_op jit(solution)/shard_map/ppermute | solution.py:19
  12.0 336.4 %reduce-scatter.7.cloned.1.call-start = ((), (), s32[]{:S(2)}) async-start(), calls=%async_computation.5 | async-start | bytes 294912 | tf_op jit(solution)/shard_map/reduce_scatter | solution.py:90
  24.4 1.0 copy-start.14
  24.4 1.3 copy-start.16
  24.4 2.5 copy-start.12
  24.4 2.6 copy-start.13
  24.4 79.8 %copy-start.11 = (f32[1,3200]{1,0:T(1,128)S(1)}, f32[1,3200]{1,0:T(1,128)}, u32[]{:S(2)}) copy-start(f32[1,3200]{1,0:T(1,128)} %param.54) | copy-start | bytes 38404
  112.0 43.3 %collective-permute-start.1 = (f32[128]{0:T(128)S(1)}, f32[128]{0:T(128)S(1)}, u32[]{:S(2)}, u32[]{:S(2)}) collective-permute-start(f32[128]{0:T(128)S(1)} %slice_bitcast_fusion.16), channel_id=1, source_target_pairs={{0,8},{8,16},{16,24},{24,32},{32,40},{40,48},{48,56},{56,64},{64,7... | collective-permute-start | bytes 1544 | tf_op jit(solution)/shard_map/ppermute | solution.py:19
  151.5 3.8 copy-start.2
  156.6 10.9 %copy-start.8 = (f32[64,25,128]{2,0,1:T(8,128)}, f32[64,25,128]{2,0,1:T(8,128)S(1)}, u32[]{:S(2)}) copy-start(f32[64,25,128]{2,0,1:T(8,128)S(1)} %get-tuple-element.281) | copy-start | bytes 2457604
  167.7 153.9 %copy-start.15 = (s32[1,128]{1,0:T(1,128)S(1)}, s32[1,128]{1,0:T(1,128)}, u32[]{:S(2)}) copy-start(s32[1,128]{1,0:T(1,128)} %param.61) | copy-start | bytes 1540
  314.6 10.5 %collective-permute-start.2 = (f32[128]{0:T(128)S(1)}, f32[128]{0:T(128)S(1)}, u32[]{:S(2)}, u32[]{:S(2)}) collective-permute-start(f32[128]{0:T(128)S(1)} %slice_bitcast_fusion.15), channel_id=1, source_target_pairs={{8,0},{16,8},{24,16},{32,24},{40,32},{48,40},{56,48},{64,56},{72,6... | collective-permute-start | bytes 1544 | tf_op jit(solution)/shard_map/ppermute | solution.py:19
  317.1 262.2 %reduce-scatter.9.cloned.1.call-start = ((), (), s32[]{:S(2)}) async-start(), calls=%async_computation.6 | async-start | bytes 294912 | tf_op jit(solution)/shard_map/reduce_scatter | solution.py:90
  351.9 0.9 copy-start.3
  354.9 30.4 %collective-permute-start.3 = (f32[128]{0:T(128)S(1)}, f32[128]{0:T(128)S(1)}, u32[]{:S(2)}, u32[]{:S(2)}) collective-permute-start(f32[128]{0:T(128)S(1)} %slice_bitcast_fusion.14), channel_id=1, source_target_pairs={{0,8},{8,16},{16,24},{24,32},{32,40},{40,48},{48,56},{56,64},{64,7... | collective-permute-start | bytes 1544 | tf_op jit(solution)/shard_map/ppermute | solution.py:19
  381.8 4.0 copy-start.9
  386.8 10.9 %copy-start.7 = (f32[64,25,128]{2,0,1:T(8,128)}, f32[64,25,128]{2,0,1:T(8,128)S(1)}, u32[]{:S(2)}) copy-start(f32[64,25,128]{2,0,1:T(8,128)S(1)} %get-tuple-element.275) | copy-start | bytes 2457604
  544.5 10.3 %collective-permute-start.4 = (f32[128]{0:T(128)S(1)}, f32[128]{0:T(128)S(1)}, u32[]{:S(2)}, u32[]{:S(2)}) collective-permute-start(f32[128]{0:T(128)S(1)} %slice_bitcast_fusion.13), channel_id=1, source_target_pairs={{8,0},{16,8},{24,16},{32,24},{40,32},{48,40},{56,48},{64,56},{72,6... | collective-permute-start | bytes 1544 | tf_op jit(solution)/shard_map/ppermute | solution.py:19
  547.0 263.9 %reduce-scatter.11.cloned.1.call-start = ((), (), s32[]{:S(2)}) async-start(), calls=%async_computation.7 | async-start | bytes 294912 | tf_op jit(solution)/shard_map/reduce_scatter | solution.py:90
  551.2 29.5 %copy-start.4 = (f32[64,25,128]{2,0,1:T(8,128)S(1)}, f32[64,25,128]{2,0,1:T(8,128)}, u32[]{:S(2)}) copy-start(f32[64,25,128]{2,0,1:T(8,128)} %copy-done.3) | copy-start | bytes 2457604
  585.1 30.5 %collective-permute-start.5 = (f32[128]{0:T(128)S(1)}, f32[128]{0:T(128)S(1)}, u32[]{:S(2)}, u32[]{:S(2)}) collective-permute-start(f32[128]{0:T(128)S(1)} %slice_bitcast_fusion.12), channel_id=1, source_target_pairs={{0,8},{8,16},{16,24},{24,32},{32,40},{40,48},{48,56},{56,64},{64,7... | collective-permute-start | bytes 1544 | tf_op jit(solution)/shard_map/ppermute | solution.py:19
  618.1 10.9 %copy-start.5 = (f32[64,25,128]{2,0,1:T(8,128)}, f32[64,25,128]{2,0,1:T(8,128)S(1)}, u32[]{:S(2)}) copy-start(f32[64,25,128]{2,0,1:T(8,128)S(1)} %get-tuple-element.271) | copy-start | bytes 2457604
  775.8 10.2 %collective-permute-start.6 = (f32[128]{0:T(128)S(1)}, f32[128]{0:T(128)S(1)}, u32[]{:S(2)}, u32[]{:S(2)}) collective-permute-start(f32[128]{0:T(128)S(1)} %slice_bitcast_fusion.11), channel_id=1, source_target_pairs={{8,0},{16,8},{24,16},{32,24},{40,32},{48,40},{56,48},{64,56},{72,6... | collective-permute-start | bytes 1544 | tf_op jit(solution)/shard_map/ppermute | solution.py:19
  817.0 31.6 %collective-permute-start.7 = (f32[128]{0:T(128)S(1)}, f32[128]{0:T(128)S(1)}, u32[]{:S(2)}, u32[]{:S(2)}) collective-permute-start(f32[128]{0:T(128)S(1)} %slice_bitcast_fusion.10), channel_id=1, source_target_pairs={{0,8},{8,16},{16,24},{24,32},{32,40},{40,48},{48,56},{56,64},{64,7... | collective-permute-start | bytes 1544 | tf_op jit(solution)/shard_map/ppermute | solution.py:19
  836.0 8.4 copy-start.10
  844.9 4.1 copy-start.6
  848.9 2.4 copy-start.1
Sparse Core Ops, SparseCore 0:
  12.1 36.2 reduce-scatter.4
  317.2 31.0 reduce-scatter.6
  547.1 32.1 reduce-scatter.8
  778.6 32.1 reduce-scatter.10
where the time goes:
time: 867 us; the launch traced here: 858 us
  blocking collectives  589 us (68%)
  matrix products  94.9 us (11%)
  waiting for transfers between devices  70.8 us (8%)
  other arithmetic  35 us (4%)
  local copies, waits for them, and re-layouts  28.8 us (3%)
  between operations  23.7 us (3%)
  starting transfers between devices  16 us (2%)
    psum x3, blocking collectives, body(): primal_total = lax.psum(primal_local, ('tm', 'region'))  262 us
    psum x3, blocking collectives, body(): capacity_grad = lax.psum(capacity_part, 'tm')  174 us
    all_gather x1, blocking collectives, body(): lax.all_gather(start_capacity[0], 'tm', axis=0, tiled=True)  76.9 us
    all_gather x4, blocking collectives, body(): lax.all_gather(primal_bar[:, 3][None], 'region', axis=0, tiled=True)  76.5 us
    reduce_scatter x4, waiting for transfers between devices, body(): lax.psum_scatter(jnp.einsum('jq,jhk->qhk', own_sources, partial_lines, pr...  70.7 us
    dot_general x4, matrix products, network_adjoint(): jnp.einsum('hil,iskl->hisk', dual_rows, weights, precision=HIGHEST_PRECIS...  40.4 us
    dot_general x4, matrix products, network_forward(): jnp.einsum('hpk,pkl->hpl', picked, flat_weights, precision=HIGHEST_PRECIS...  31.7 us
  transfers between devices with their start and end apart: 12, of which 3 were waited for; matrix products, arithmetic and copies ran while one was open for 11% of the time, Pallas kernels for 0%

commit v1 on v0

v1 whole, which is shorter than its diff:
```python
import functools
import math

import jax
import jax.numpy as jnp
from jax import lax
from jax.experimental import pallas as pl
from jax.experimental.pallas import tpu as pltpu
from jax.sharding import PartitionSpec as P

ITERS = 4
STEP_SCALE = 0.2
EPSILON = 1e-06
HIGHEST = lax.Precision.HIGHEST
MESH = pl.DeviceIdType.MESH
F32 = jnp.float32
BF16 = jnp.bfloat16
LOW = float(jnp.finfo(jnp.float32).min)
LANES = 128


def split(value):
    high = value.astype(BF16)
    low = (value - high.astype(F32)).astype(BF16)
    return jnp.concatenate([high, low], axis=0)


def dot_nt(a, b, precision=None):
    return lax.dot_general(
        a, b, (((1,), (1,)), ((), ())), precision=precision, preferred_element_type=F32
    )


def kernel(
    sizes,
    cols_s,
    src_s,
    cap_s,
    build_s,
    gm_v,
    unit_v,
    x_hbm,
    dem_hbm,
    w_hbm,
    lw_hbm,
    x_out,
    y_out,
    cap_out,
    xst,
    dst,
    wst,
    lw,
    wh,
    wl,
    xs,
    ys,
    grad,
    xb,
    yb,
    seg,
    extra,
    table_v,
    table_s,
    rank_v,
    rank_s,
    line_a,
    line_u,
    vx,
    gat0,
    gat,
    pbuf,
    rbuf,
    mt,
    tbuf,
    mr,
    sbuf,
    nb_src,
    nb_dst,
    load_sem,
    w_sem,
    out_sem,
    send_t,
    recv_t,
    send_r,
    recv_r,
    send_g,
    recv_g,
    send_p,
    recv_p,
    send_n,
    recv_n,
):
    (hours, cb, bs, s_count, nl, nt, nr) = sizes
    pairs = cb * s_count
    me_t = lax.axis_index("tm")
    me_r = lax.axis_index("region")
    primal_count = hours * nt * nr * cb * bs + nr * LANES
    dual_count = hours * nt * nr * cb * bs
    couple = 1.0 / math.sqrt(hours * nt)

    cx = pltpu.make_async_copy(x_hbm, xst, load_sem.at[0])
    cd = pltpu.make_async_copy(dem_hbm, dst, load_sem.at[1])
    cl = pltpu.make_async_copy(lw_hbm, lw, load_sem.at[2])
    cx.start()

    barrier = pltpu.get_barrier_semaphore()

    def offset_of(step, count):
        half = (step + 1) // 2
        return count // 2 + jnp.where(step % 2 == 1, half, -half)

    @pl.loop(0, nt - 1)
    def _(step):
        k = offset_of(step, nt)
        pl.semaphore_signal(
            barrier, inc=1, device_id=(lax.rem(me_t + k, nt), me_r), device_id_type=MESH
        )

    @pl.loop(0, nr - 1)
    def _(step):
        k = offset_of(step, nr)
        pl.semaphore_signal(
            barrier, inc=1, device_id=(me_t, lax.rem(me_r + k, nr)), device_id_type=MESH
        )

    cd.start()
    cl.start()
    w_copies = [
        pltpu.make_async_copy(w_hbm.at[i], wst.at[i], w_sem.at[i]) for i in range(cb)
    ]
    for c in w_copies:
        c.start()

    lane = lax.broadcasted_iota(jnp.int32, (1, LANES), 1)
    col_vec = jnp.full((1, LANES), cb, jnp.int32)
    for p in range(pairs):
        col_vec = jnp.where(lane == p, cols_s[p], col_vec)
    rank = jnp.zeros((1, LANES), jnp.int32)
    end_vec = jnp.zeros((1, LANES), jnp.int32)
    for q in range(pairs):
        c = cols_s[q]
        ahead = (col_vec > c) | ((col_vec == c) & (lane > q))
        rank = rank + jnp.where(ahead, 1, 0)
        end_vec = end_vec + jnp.where(lane >= c, 1, 0)
    start_vec = jnp.where(lane == 0, 0, pltpu.roll(end_vec, 1, 1))
    rank_v[...] = rank
    c1 = pltpu.make_async_copy(rank_v, rank_s, load_sem.at[3])
    c1.start()

    own_n = LANES // nt
    cap_vec = jnp.zeros((1, LANES), F32)
    build_vec = jnp.zeros((1, LANES), F32)
    for k in range(own_n):
        here = lane == me_t * own_n + k
        cap_vec = jnp.where(here, cap_s[0, k], cap_vec)
        build_vec = jnp.where(here, build_s[0, k], build_vec)
    mt[0, :, 0:LANES] = cap_vec
    mt[0, :, LANES : 2 * LANES] = build_vec

    cx.wait()
    vx[0:hours, :] = xst[pl.ds(3, hours, stride=cb), :]
    vx[hours : hours + 8, :] = jnp.broadcast_to(unit_v[3], (8, LANES))
    nb_src[0] = xst[pl.ds((hours - 1) * cb, 1), :]

    sel_t = jnp.where(
        gm_v[...] == lax.broadcasted_iota(jnp.int32, (LANES, LANES), 0), 1.0, 0.0
    ).astype(F32)

    pl.semaphore_wait(barrier, nt - 1 + nr - 1)

    def tm_send(r):
        @pl.loop(0, nt - 1)
        def _(step):
            k = offset_of(step, nt)
            pltpu.make_async_remote_copy(
                src_ref=mt.at[r],
                dst_ref=tbuf.at[r, k - 1],
                send_sem=send_t.at[r],
                recv_sem=recv_t.at[r],
                device_id=(lax.rem(me_t + k, nt), me_r),
                device_id_type=MESH,
            ).start()

    def tm_sum(r):
        pltpu.make_async_copy(tbuf.at[r], tbuf.at[r], recv_t.at[r]).wait()
        total = mt[r]
        for k in range(nt - 1):
            total = total + tbuf[r, k]
        return total

    def region_send(src, dst_of, send_sem, recv_sem):
        @pl.loop(0, nr - 1)
        def _(step):
            k = offset_of(step, nr)
            pltpu.make_async_remote_copy(
                src_ref=src(k),
                dst_ref=dst_of(k),
                send_sem=send_sem,
                recv_sem=recv_sem,
                device_id=(me_t, lax.rem(me_r + k, nr)),
                device_id_type=MESH,
            ).start()

    def to_next(n, r, by):
        pltpu.make_async_remote_copy(
            src_ref=nb_src.at[n],
            dst_ref=nb_dst.at[n],
            send_sem=send_n.at[n],
            recv_sem=recv_n.at[n],
            device_id=(lax.rem(me_t + nt + by, nt), me_r),
            device_id_type=MESH,
        ).start()

    def next_wait(n):
        pltpu.make_async_copy(nb_dst.at[n], nb_dst.at[n], recv_n.at[n]).wait()

    region_send(
        lambda k: vx, lambda k: gat0.at[me_r], send_g.at[0], recv_g.at[0]
    )
    tm_send(0)
    to_next(0, 0, 1)
    gat0[me_r] = vx[...]

    def primal_block(c, x, g, step):
        low = jnp.where(c == 3, LOW, 0.0)
        new = jnp.maximum(x - step * g, low)
        change = new - x
        bar = new + change
        xs[c] = new
        xb[c] = split(bar)
        return bar, change * change

    def fold(sq):
        return jnp.sum(sq.reshape(hours // 8, 8, LANES), axis=0)

    c1.wait()
    order = jnp.zeros((1, LANES), jnp.int32)
    order_row = jnp.zeros((1, LANES), jnp.int32)
    order_col = jnp.full((1, LANES), -1, jnp.int32)
    for p in range(pairs):
        here = lane == rank_s[0, p]
        order = jnp.where(here, p, order)
        order_row = jnp.where(here, p // s_count, order_row)
        order_col = jnp.where(here, cols_s[p], order_col)
    goes_on = (order_col == pltpu.roll(order_col, 1, 1)) & (lane > 0)
    table_v[0:1, :] = order
    table_v[1:2, :] = order_row
    table_v[2:3, :] = jnp.where(goes_on, 1, 0)
    table_v[3:4, :] = jnp.maximum(end_vec - 1, 0)
    table_v[4:5, :] = jnp.where(end_vec > start_vec, 1, 0)
    table_v[5:8, :] = jnp.zeros((3, LANES), jnp.int32)
    c2 = pltpu.make_async_copy(table_v, table_s, load_sem.at[4])
    c2.start()

    for i in range(cb):
        w_copies[i].wait()

        @pl.loop(0, s_count)
        def _(s, i=i):
            w = wst[i, s]
            high = w.astype(BF16)
            wh[i * s_count + s] = high
            wl[i * s_count + s] = (w - high.astype(F32)).astype(BF16)

    first_step = STEP_SCALE

    def first_primal(c, acc):
        x = xst[pl.ds(c, hours, stride=cb), :]
        g = jnp.broadcast_to(unit_v[c], (hours, LANES))
        bar, sq = primal_block(c, x, g, first_step)
        return bar, acc + fold(sq)

    zero8 = jnp.zeros((8, LANES), F32)
    bar0, sq_p = first_primal(0, zero8)
    sq_p = lax.fori_loop(1, cb, lambda c, a: first_primal(c, a)[1], sq_p)

    def network(i):
        x3 = jnp.concatenate([xb[cols_s[i * s_count + s]] for s in range(s_count)], axis=1)
        high = jnp.concatenate([wh[i * s_count + s] for s in range(s_count)], axis=0)
        low = jnp.concatenate([wl[i * s_count + s] for s in range(s_count)], axis=0)
        both = jnp.dot(x3, high, preferred_element_type=F32)
        last = jnp.dot(x3[0:hours], low, preferred_element_type=F32)
        return both[0:hours] + both[hours:] + last

    def dual_block(i, target, step, first):
        low = jnp.where(i < 3, LOW, 0.0)
        move = step * (target - network(i))
        if first:
            new = jnp.maximum(move, low)
            change = new
        else:
            old = ys[i]
            new = jnp.maximum(old + move, low)
            change = new - old
        ys[i] = new
        yb[i] = split(new)
        return fold(change * change)

    def target_of(i):
        return dst[pl.ds(i, hours, stride=cb), :]

    def line_apply(block_of):
        parts = jnp.concatenate([block_of(src_s[me_r * nl + j]) for j in range(nl)], axis=1)
        return jnp.dot(parts, lw[...], precision=HIGHEST, preferred_element_type=F32)

    row = lax.broadcasted_iota(jnp.int32, (hours, LANES), 0)
    has_before = jnp.where(me_t > 0, 1.0, 0.0).astype(F32)
    has_after = jnp.where(me_t < nt - 1, 1.0, 0.0).astype(F32)

    def forward(bar0, prev_bar, cap_bar, line_flow, step, first):
        def plain(i, a):
            return a + dual_block(i, target_of(i), step, first)

        sq = lax.fori_loop(3, cb, plain, zero8)
        earlier = pltpu.roll(bar0, 1, 0)
        earlier = jnp.where(row == 0, prev_bar * has_before, earlier)
        extra[0] = target_of(0) + earlier
        picked = jnp.dot(
            jnp.broadcast_to(cap_bar(), (8, LANES)),
            sel_t,
            precision=HIGHEST,
            preferred_element_type=F32,
        )[0:1]
        extra[2] = target_of(2) - couple * picked
        extra[1] = target_of(1) - line_flow()

        def special(i, a):
            return a + dual_block(i, extra[i], step, first)

        return lax.fori_loop(0, 3, special, sq)

    lane_low = lane < LANES // 2

    def pack(p, d):
        p = jnp.sum(p, axis=0, keepdims=True)
        d = jnp.sum(d, axis=0, keepdims=True)
        p = p + pltpu.roll(p, LANES // 2, 1)
        d = d + pltpu.roll(d, LANES // 2, 1)
        return jnp.where(lane_low, p, d)

    cl.wait()
    cd.wait()
    gathered = []

    def first_capacity():
        total = tm_sum(0)
        cap = total[:, 0:LANES]
        build = total[:, LANES : 2 * LANES]
        new_cap = jnp.maximum(cap - first_step * build, 0.0)
        gathered.extend([cap, build, new_cap])
        return new_cap + (new_cap - cap)

    def first_flow():
        pltpu.make_async_copy(
            gat0.at[pl.ds(0, nr - 1)], gat0.at[pl.ds(0, nr - 1)], recv_g.at[0]
        ).wait()
        both = line_apply(lambda q: gat0[q])
        line_unit = both[hours : hours + 1]
        line_x = both[0:hours]
        line_u[...] = jnp.broadcast_to(line_unit, (8, LANES))
        new_line = line_x - first_step * line_unit
        line_a[...] = new_line
        return new_line - first_step * line_unit

    next_wait(0)
    prev_old = nb_dst[0]
    prev_new = jnp.maximum(prev_old - first_step * unit_v[0], 0.0)
    prev_bar = prev_new + (prev_new - prev_old)
    sq_d = forward(bar0, prev_bar, first_capacity, first_flow, first_step, True)
    cap_old, build, cap_new = gathered

    c2.wait()

    def later(it, carry):
        prev_x, cap, cap_change, weight, sq_p, sq_d = carry
        r = it - 1
        mt[it, :, 0:LANES] = jnp.sum(ys[2], axis=0, keepdims=True)
        mt[it, :, LANES : 2 * LANES] = pack(sq_p, sq_d)
        nb_src[1 + r] = ys[0, 0:1, :]
        tm_send(it)
        to_next(1 + r, r, -1)

        terms = dot_nt(ys[1], lw[...].reshape(nl * bs, bs), precision=HIGHEST)
        for k in range(nr):
            q = lax.rem(me_r + k, nr)
            total = jnp.zeros((hours, LANES), F32)
            for j in range(nl):
                on = jnp.where(src_s[me_r * nl + j] == q, 1.0, 0.0).astype(F32)
                total = total + on * terms[:, j * bs : (j + 1) * bs]
            pbuf[r, k] = total
        region_send(
            lambda k: pbuf.at[r, k], lambda k: rbuf.at[r, k - 1], send_p.at[r], recv_p.at[r]
        )

        def pair(n, total):
            p = table_s[0, n]
            y = yb[table_s[1, n]]
            keep = table_s[2, n].astype(F32)
            both = dot_nt(y, wh[p])
            low = dot_nt(y[0:hours], wl[p])
            total = keep * total + (both[0:hours] + both[hours:] + low)
            seg[n] = total
            return total

        lax.fori_loop(0, pairs, pair, jnp.zeros((hours, LANES), F32))

        def gradient(c, _):
            grad[c] = unit_v[c] - table_s[4, c].astype(F32) * seg[table_s[3, c]]
            return 0

        lax.fori_loop(0, cb, gradient, 0)
        nb_src[4 + r] = grad[0, hours - 1 : hours, :]
        to_next(4 + r, r, 1)

        next_wait(1 + r)
        following = pltpu.roll(ys[0], hours - 1, 0)
        following = jnp.where(row == hours - 1, nb_dst[1 + r] * has_after, following)
        grad[0] = grad[0] + following

        total = tm_sum(it)
        col_sums = total[:, 0:LANES]
        region_sums = total[:, LANES : 2 * LANES] + pack(
            cap_change, jnp.zeros_like(cap_change)
        )
        mr[r] = region_sums
        region_send(
            lambda k: mr.at[r], lambda k: sbuf.at[r, k - 1], send_r.at[r], recv_r.at[r]
        )
        capacity_grad = couple * dot_nt(
            jnp.broadcast_to(col_sums, (8, LANES)), sel_t, precision=HIGHEST
        )[0:1]

        pltpu.make_async_copy(rbuf.at[r], rbuf.at[r], recv_p.at[r]).wait()
        line_back = pbuf[r, 0]
        for k in range(nr - 1):
            line_back = line_back + rbuf[r, k]
        flow_grad = grad[3] - line_back
        grad[3] = flow_grad
        gat[r, me_r] = flow_grad
        region_send(
            lambda k: gat.at[r, me_r],
            lambda k: gat.at[r, me_r],
            send_g.at[it],
            recv_g.at[it],
        )
        next_wait(4 + r)
        prev_grad = nb_dst[4 + r] + ys[0, 0:1, :]

        pltpu.make_async_copy(sbuf.at[r], sbuf.at[r], recv_r.at[r]).wait()
        sums = mr[r]
        for k in range(nr - 1):
            sums = sums + sbuf[r, k]
        total_p = jnp.sum(jnp.where(lane_low, sums, 0.0), axis=1, keepdims=True)
        total_d = jnp.sum(jnp.where(lane_low, 0.0, sums), axis=1, keepdims=True)
        total_p = jnp.broadcast_to(total_p, (1, LANES))
        total_d = jnp.broadcast_to(total_d, (1, LANES))
        weight = jnp.sqrt(
            weight
            * jnp.sqrt(total_p / primal_count + EPSILON)
            / jnp.sqrt(total_d / dual_count + EPSILON)
        )
        primal_step = STEP_SCALE / weight
        dual_step = STEP_SCALE * weight

        def primal(c, a):
            bar, sq = primal_block(c, xs[c], grad[c], primal_step)
            return bar, a + fold(sq)

        bar0, sq_p = primal(0, zero8)
        sq_p = lax.fori_loop(1, cb, lambda c, a: primal(c, a)[1], sq_p)
        new_cap = jnp.maximum(cap - primal_step * (build - capacity_grad), 0.0)
        cap_diff = new_cap - cap
        prev_new = jnp.maximum(prev_x - primal_step * prev_grad, 0.0)
        prev_bar = prev_new + (prev_new - prev_x)

        def flow():
            pltpu.make_async_copy(
                gat.at[r, pl.ds(0, nr - 1)], gat.at[r, pl.ds(0, nr - 1)], recv_g.at[it]
            ).wait()
            line_grad = line_apply(lambda q: gat[r, q])
            new_line = line_a[...] - primal_step * line_grad
            line_a[...] = new_line
            return new_line - primal_step * line_grad

        sq_d = forward(bar0, prev_bar, lambda: new_cap + cap_diff, flow, dual_step, False)
        return prev_new, new_cap, cap_diff * cap_diff, weight, sq_p, sq_d

    first_diff = cap_new - cap_old
    carry = (
        prev_new,
        cap_new,
        first_diff * first_diff,
        jnp.ones((1, LANES), F32),
        sq_p,
        sq_d,
    )
    carry = lax.fori_loop(1, ITERS, later, carry)
    cap_out[...] = carry[1]

    def write(c, _):
        xst[pl.ds(c, hours, stride=cb), :] = xs[c]
        dst[pl.ds(c, hours, stride=cb), :] = ys[c]
        return 0

    lax.fori_loop(0, cb, write, 0)
    ox = pltpu.make_async_copy(xst, x_out, out_sem.at[0])
    oy = pltpu.make_async_copy(dst, y_out, out_sem.at[1])
    ox.start()
    oy.start()

    for r in range(ITERS):
        for k in range(nt - 1):
            pltpu.make_async_copy(mt.at[r], mt.at[r], send_t.at[r]).wait()
    pltpu.make_async_copy(
        gat0.at[pl.ds(0, nr - 1)], gat0.at[pl.ds(0, nr - 1)], send_g.at[0]
    ).wait()
    for r in range(ITERS - 1):
        pltpu.make_async_copy(sbuf.at[r], sbuf.at[r], send_r.at[r]).wait()
        pltpu.make_async_copy(rbuf.at[r], rbuf.at[r], send_p.at[r]).wait()
        pltpu.make_async_copy(
            gat.at[r, pl.ds(0, nr - 1)], gat.at[r, pl.ds(0, nr - 1)], send_g.at[r + 1]
        ).wait()
    for n in range(1 + 2 * (ITERS - 1)):
        pltpu.make_async_copy(nb_src.at[n], nb_src.at[n], send_n.at[n]).wait()
    ox.wait()
    oy.wait()


def body(
    start_primal,
    demand,
    unit_cost,
    build_cost,
    start_capacity,
    net_weights,
    net_columns,
    line_weights,
    line_source,
    generator_map,
):
    hours, _, width = start_primal.shape
    bs = net_weights.shape[3]
    cb = width // bs
    s_count = net_weights.shape[2]
    nl = line_weights.shape[1]
    nt = lax.axis_size("tm")
    nr = lax.axis_size("region")
    pairs = cb * s_count
    sizes = (hours, cb, bs, s_count, nl, nt, nr)
    smem = pl.BlockSpec(memory_space=pltpu.SMEM)
    vmem = pl.BlockSpec(memory_space=pltpu.VMEM)
    hbm = pl.BlockSpec(memory_space=pl.ANY)
    rounds = ITERS - 1
    dma = pltpu.SemaphoreType.DMA
    x_new, y_new, cap = pl.pallas_call(
        functools.partial(kernel, sizes),
        out_shape=(
            jax.ShapeDtypeStruct((hours * cb, bs), F32),
            jax.ShapeDtypeStruct((hours * cb, bs), F32),
            jax.ShapeDtypeStruct((1, LANES), F32),
        ),
        in_specs=[smem] * 4 + [vmem] * 2 + [hbm] * 4,
        out_specs=(hbm, hbm, vmem),
        scratch_shapes=[
            pltpu.VMEM((hours * cb, bs), F32),
            pltpu.VMEM((hours * cb, bs), F32),
            pltpu.VMEM((cb, s_count, bs, bs), F32),
            pltpu.VMEM((nl * bs, bs), F32),
            pltpu.VMEM((pairs, bs, bs), BF16),
            pltpu.VMEM((pairs, bs, bs), BF16),
            pltpu.VMEM((cb, hours, bs), F32),
            pltpu.VMEM((cb, hours, bs), F32),
            pltpu.VMEM((cb, hours, bs), F32),
            pltpu.VMEM((cb, 2 * hours, bs), BF16),
            pltpu.VMEM((cb, 2 * hours, bs), BF16),
            pltpu.VMEM((pairs, hours, bs), F32),
            pltpu.VMEM((3, hours, bs), F32),
            pltpu.VMEM((8, LANES), jnp.int32),
            pltpu.SMEM((8, LANES), jnp.int32),
            pltpu.VMEM((1, LANES), jnp.int32),
            pltpu.SMEM((1, LANES), jnp.int32),
            pltpu.VMEM((hours, bs), F32),
            pltpu.VMEM((8, bs), F32),
            pltpu.VMEM((hours + 8, bs), F32),
            pltpu.VMEM((nr, hours + 8, bs), F32),
            pltpu.VMEM((rounds, nr, hours, bs), F32),
            pltpu.VMEM((rounds, nr, hours, bs), F32),
            pltpu.VMEM((rounds, nr - 1, hours, bs), F32),
            pltpu.VMEM((ITERS, 1, 2 * LANES), F32),
            pltpu.VMEM((ITERS, nt - 1, 1, 2 * LANES), F32),
            pltpu.VMEM((rounds, 1, LANES), F32),
            pltpu.VMEM((rounds, nr - 1, 1, LANES), F32),
            pltpu.VMEM((1 + 2 * rounds, 1, LANES), F32),
            pltpu.VMEM((1 + 2 * rounds, 1, LANES), F32),
            dma((5,)),
            dma((cb,)),
            dma((2,)),
            dma((ITERS,)),
            dma((ITERS,)),
            dma((rounds,)),
            dma((rounds,)),
            dma((ITERS,)),
            dma((ITERS,)),
            dma((rounds,)),
            dma((rounds,)),
            dma((1 + 2 * rounds,)),
            dma((1 + 2 * rounds,)),
        ],
        compiler_params=pltpu.CompilerParams(collective_id=0, has_side_effects=True),
    )(
        net_columns.reshape(pairs),
        line_source.reshape(-1),
        start_capacity,
        build_cost,
        generator_map,
        unit_cost.reshape(cb, 1, bs),
        start_primal.reshape(hours * cb, bs),
        demand.reshape(hours * cb, bs),
        net_weights[0],
        line_weights.reshape(nl * bs, bs),
    )
    own = start_capacity.shape[1]
    capacity = lax.dynamic_slice_in_dim(cap, lax.axis_index("tm") * own, own, 1)
    return (
        x_new.reshape(hours, 1, width),
        y_new.reshape(hours, 1, width),
        capacity,
    )


def solution(mesh):
    in_specs = (
        P("tm", "region", None),
        P("tm", "region", None),
        P("region", None),
        P("region", "tm"),
        P("region", "tm"),
        P("region", None, None, None, None),
        P("region", None, None),
        P("region", None, None, None),
        P(),
        P("region", None),
    )
    out_specs = (P("tm", "region", None), P("tm", "region", None), P("region", "tm"))
    return jax.shard_map(body, mesh=mesh, in_specs=in_specs, out_specs=out_specs, check_vma=False)
```

time: 867 us -> 105 us (0.12)
  blocking collectives: 589 us -> 0 us
  Pallas kernels: 0 us -> 95.7 us
  matrix products: 94.9 us -> 0 us
  waiting for transfers between devices: 70.8 us -> 0 us
  other arithmetic: 35 us -> 0 us
  between operations: 23.7 us -> 0.65 us
  local copies, waits for them, and re-layouts: 28.8 us -> 8.22 us
  starting transfers between devices: 16 us -> 0 us
    psum x6 -> x0, blocking collectives: 436 us -> none  [the longest x3 262 us: body(): primal_total = lax.psum(primal_local, ('tm', 'region'))]
    all_gather x5 -> x0, blocking collectives: 153 us -> none  [the longest x1 76.9 us: body(): lax.all_gather(start_capacity[0], 'tm', axis=0, tiled=True)]
    pallas_call x0 -> x1, Pallas kernels: none -> 95.7 us  [body(): pl.pallas_call(functools.partial(kernel, sizes), out_shape=(jax.ShapeDtyp...]
    dot_general x36 -> x0, matrix products: 94.9 us -> none  [the longest x4 40.4 us: network_adjoint(): jnp.einsum('hil,iskl->hisk', dual_rows, weights, precision=HIGHEST_PRECIS...]
    reduce_scatter x4 -> x0, waiting for transfers between devices: 70.7 us -> none  [body(): lax.psum_scatter(jnp.einsum('jq,jhk->qhk', own_sources, partial_lines, pr...]
    reduce_sum x16 -> x0, other arithmetic: 19.8 us -> none  [the longest x4 8.06 us: network_forward(): product.reshape(hour_count, columns.shape[0], columns.shape[1], -1)]
    ppermute x8 -> x0, starting transfers between devices: 15.3 us -> none  [shifted(): return lax.ppermute(shard, axis, pairs)]
    dot_general x12 -> x0, local copies, waits for them, and re-layouts: 9.5 us -> none  [the longest x8 6.5 us: network_adjoint(): jnp.einsum('hpk,pc->hck', stacked, placing, precision=HIGHEST_PRECISION)]
  transfers between devices with their start and end apart: 12 -> 0, of which waited for: 3 -> 0; matrix products, arithmetic and copies ran while one was open for 11% -> 0% of each run, Pallas kernels for 0% -> 0%
where the time goes in v1:
time: 105 us
  Pallas kernels  95.7 us (91%)
  local copies, waits for them, and re-layouts  8.22 us (8%)
    pallas_call x1, Pallas kernels, body(): pl.pallas_call(functools.partial(kernel, sizes), out_shape=(jax.ShapeDtyp...  95.7 us
    unnamed x4, local copies, waits for them, and re-layouts  5.74 us

profile of v1, /device:TPU:1, one launch (start us, length us, event | category | flops | bytes accessed | tf_op | source)
XLA Modules:
  0.0 104.5 jit_solution(9491154516638936705)
XLA Ops:
  0.6 0.8 copy.18
  1.4 0.6 reshape.31.src_s
  2.0 0.8 copy.17
  2.8 0.6 reshape.30.cols_s
  3.4 95.7 %shard_map.121 = (f32[1600,128]{1,0:T(8,128)}, f32[1600,128]{1,0:T(8,128)}, f32[1,128]{1,0:T(1,128)}) custom-call(s32[75]{0:T(128)} %reshape.30.cols_s, s32[32]{0:T(128)} %reshape.31.src_s, f32[1,4]{1,0:T(1,128)} %cap_s.1, f32[1,4]{1,0:T(1,128)} %build_s.1, s32[1,128]{1,0:T(1,128)} %gm_v.1, f32[25,1,128]{2,1,0:T(1,128)} %bitcast.13, f32[1600,128]{1,0:T(8,128)} %bitcast.8, ...), custom_call_target="tpu_custom_call" | custom-call | tf_op jit(solution)/shard_map/pallas_call | solution.py:555
  99.1 1.3 %constant_dynamic-slice_fusion = f32[1,4]{1,0:T(1,128)} fusion(f32[1,128]{1,0:T(1,128)} %get-tuple-element.8, s32[]{:T(128)S(6)} %select_n.3), kind=kLoop, calls=%fused_computation | loop fusion | bytes 36 | tf_op jit(solution)/shard_map/dynamic_slice | solution.py:623
  100.3 2.1 %copy.23 = f32[64,1,3200]{2,1,0:T(1,128)} copy(f32[64,1,3200]{2,1,0:T(1,128)} %bitcast.11) | data formatting | bytes 1638400
  102.4 2.1 %copy.24 = f32[64,1,3200]{2,1,0:T(1,128)} copy(f32[64,1,3200]{2,1,0:T(1,128)} %bitcast.10) | data formatting | bytes 1638400

commit v2 on v1

--- a/solution.py
+++ b/solution.py
@@ -23,6 +23,17 @@
     high = value.astype(BF16)
     low = (value - high.astype(F32)).astype(BF16)
     return jnp.concatenate([high, low], axis=0)
+
+
+def unrolled(first, last, by, step, carry):
+    assert (last - first) % by == 0
+
+    def some(n, c):
+        for k in range(by):
+            c = step(first + n * by + k, c)
+        return c
+
+    return lax.fori_loop(0, (last - first) // by, some, carry)
 
 
 def dot_nt(a, b, precision=None):
@@ -106,21 +117,25 @@
     barrier = pltpu.get_barrier_semaphore()
 
     def offset_of(step, count):
-        half = (step + 1) // 2
-        return count // 2 + jnp.where(step % 2 == 1, half, -half)
+        k = step + count // 2
+        return jnp.where(k >= count, k - (count - 1), k)
+
+    def around(me, k, count):
+        at = me + k
+        return jnp.where(at >= count, at - count, at)
 
     @pl.loop(0, nt - 1)
     def _(step):
         k = offset_of(step, nt)
         pl.semaphore_signal(
-            barrier, inc=1, device_id=(lax.rem(me_t + k, nt), me_r), device_id_type=MESH
+            barrier, inc=1, device_id=(around(me_t, k, nt), me_r), device_id_type=MESH
         )
 
     @pl.loop(0, nr - 1)
     def _(step):
         k = offset_of(step, nr)
         pl.semaphore_signal(
-            barrier, inc=1, device_id=(me_t, lax.rem(me_r + k, nr)), device_id_type=MESH
+            barrier, inc=1, device_id=(me_t, around(me_r, k, nr)), device_id_type=MESH
         )
 
     cd.start()
@@ -132,13 +147,17 @@
         c.start()
 
     lane = lax.broadcasted_iota(jnp.int32, (1, LANES), 1)
+
+    def column(p):
+        return cols_s[p % s_count, 0, p // s_count]
+
     col_vec = jnp.full((1, LANES), cb, jnp.int32)
     for p in range(pairs):
-        col_vec = jnp.where(lane == p, cols_s[p], col_vec)
+        col_vec = jnp.where(lane == p, column(p), col_vec)
     rank = jnp.zeros((1, LANES), jnp.int32)
     end_vec = jnp.zeros((1, LANES), jnp.int32)
     for q in range(pairs):
-        c = cols_s[q]
+        c = column(q)
         ahead = (col_vec > c) | ((col_vec == c) & (lane > q))
         rank = rank + jnp.where(ahead, 1, 0)
         end_vec = end_vec + jnp.where(lane >= c, 1, 0)
@@ -166,6 +185,38 @@
         gm_v[...] == lax.broadcasted_iota(jnp.int32, (LANES, LANES), 0), 1.0, 0.0
     ).astype(F32)
 
+    c1.wait()
+    order = jnp.zeros((1, LANES), jnp.int32)
+    order_row = jnp.zeros((1, LANES), jnp.int32)
+    order_col = jnp.full((1, LANES), -1, jnp.int32)
+    for p in range(pairs):
+        here = lane == rank_s[0, p]
+        order = jnp.where(here, p, order)
+        order_row = jnp.where(here, p // s_count, order_row)
+        order_col = jnp.where(here, column(p), order_col)
+    goes_on = (order_col == pltpu.roll(order_col, 1, 1)) & (lane > 0)
+    table_v[0:1, :] = order
+    table_v[1:2, :] = order_row
+    table_v[2:3, :] = jnp.where(goes_on, 1, 0)
+    table_v[3:4, :] = jnp.maximum(end_vec - 1, 0)
+    table_v[4:5, :] = jnp.where(end_vec > start_vec, 1, 0)
+    table_v[5:8, :] = jnp.zeros((3, LANES), jnp.int32)
+    c2 = pltpu.make_async_copy(table_v, table_s, load_sem.at[4])
+    c2.start()
+
+    def split_weights(i):
+        w_copies[i].wait()
+
+        @pl.loop(0, s_count)
+        def _(s):
+            w = wst[i, s]
+            high = w.astype(BF16)
+            wh[i * s_count + s] = high
+            wl[i * s_count + s] = (w - high.astype(F32)).astype(BF16)
+
+    for i in range(cb // 2):
+        split_weights(i)
+
     pl.semaphore_wait(barrier, nt - 1 + nr - 1)
 
     def tm_send(r):
@@ -177,7 +228,7 @@
                 dst_ref=tbuf.at[r, k - 1],
                 send_sem=send_t.at[r],
                 recv_sem=recv_t.at[r],
-                device_id=(lax.rem(me_t + k, nt), me_r),
+                device_id=(around(me_t, k, nt), me_r),
                 device_id_type=MESH,
             ).start()
 
@@ -197,7 +248,7 @@
                 dst_ref=dst_of(k),
                 send_sem=send_sem,
                 recv_sem=recv_sem,
-                device_id=(me_t, lax.rem(me_r + k, nr)),
+                device_id=(me_t, around(me_r, k, nr)),
                 device_id_type=MESH,
             ).start()
 
@@ -207,7 +258,7 @@
             dst_ref=nb_dst.at[n],
             send_sem=send_n.at[n],
             recv_sem=recv_n.at[n],
-            device_id=(lax.rem(me_t + nt + by, nt), me_r),
+            device_id=(around(me_t, (by + nt) % nt, nt), me_r),
             device_id_type=MESH,
         ).start()
 
@@ -233,34 +284,8 @@
     def fold(sq):
         return jnp.sum(sq.reshape(hours // 8, 8, LANES), axis=0)
 
-    c1.wait()
-    order = jnp.zeros((1, LANES), jnp.int32)
-    order_row = jnp.zeros((1, LANES), jnp.int32)
-    order_col = jnp.full((1, LANES), -1, jnp.int32)
-    for p in range(pairs):
-        here = lane == rank_s[0, p]
-        order = jnp.where(here, p, order)
-        order_row = jnp.where(here, p // s_count, order_row)
-        order_col = jnp.where(here, cols_s[p], order_col)
-    goes_on = (order_col == pltpu.roll(order_col, 1, 1)) & (lane > 0)
-    table_v[0:1, :] = order
-    table_v[1:2, :] = order_row
-    table_v[2:3, :] = jnp.where(goes_on, 1, 0)
-    table_v[3:4, :] = jnp.maximum(end_vec - 1, 0)
-    table_v[4:5, :] = jnp.where(end_vec > start_vec, 1, 0)
-    table_v[5:8, :] = jnp.zeros((3, LANES), jnp.int32)
-    c2 = pltpu.make_async_copy(table_v, table_s, load_sem.at[4])
-    c2.start()
-
-    for i in range(cb):
-        w_copies[i].wait()
-
-        @pl.loop(0, s_count)
-        def _(s, i=i):
-            w = wst[i, s]
-            high = w.astype(BF16)
-            wh[i * s_count + s] = high
-            wl[i * s_count + s] = (w - high.astype(F32)).astype(BF16)
+    for i in range(cb // 2, cb):
+        split_weights(i)
 
     first_step = STEP_SCALE
 
@@ -272,10 +297,10 @@
 
     zero8 = jnp.zeros((8, LANES), F32)
     bar0, sq_p = first_primal(0, zero8)
-    sq_p = lax.fori_loop(1, cb, lambda c, a: first_primal(c, a)[1], sq_p)
+    sq_p = unrolled(1, cb, 4, lambda c, a: first_primal(c, a)[1], sq_p)
 
     def network(i):
-        x3 = jnp.concatenate([xb[cols_s[i * s_count + s]] for s in range(s_count)], axis=1)
+        x3 = jnp.concatenate([xb[cols_s[s, 0, i]] for s in range(s_count)], axis=1)
         high = jnp.concatenate([wh[i * s_count + s] for s in range(s_count)], axis=0)
         low = jnp.concatenate([wl[i * s_count + s] for s in range(s_count)], axis=0)
         both = jnp.dot(x3, high, preferred_element_type=F32)
@@ -300,7 +325,7 @@
         return dst[pl.ds(i, hours, stride=cb), :]
 
     def line_apply(block_of):
-        parts = jnp.concatenate([block_of(src_s[me_r * nl + j]) for j in range(nl)], axis=1)
+        parts = jnp.concatenate([block_of(src_s[j, me_r]) for j in range(nl)], axis=1)
         return jnp.dot(parts, lw[...], precision=HIGHEST, preferred_element_type=F32)
 
     row = lax.broadcasted_iota(jnp.int32, (hours, LANES), 0)
@@ -311,7 +336,7 @@
         def plain(i, a):
             return a + dual_block(i, target_of(i), step, first)
 
-        sq = lax.fori_loop(3, cb, plain, zero8)
+        sq = unrolled(3, cb, 11, plain, zero8)
         earlier = pltpu.roll(bar0, 1, 0)
         earlier = jnp.where(row == 0, prev_bar * has_before, earlier)
         extra[0] = target_of(0) + earlier
@@ -322,12 +347,10 @@
             preferred_element_type=F32,
         )[0:1]
         extra[2] = target_of(2) - couple * picked
+        sq = sq + dual_block(0, extra[0], step, first)
+        sq = sq + dual_block(2, extra[2], step, first)
         extra[1] = target_of(1) - line_flow()
-
-        def special(i, a):
-            return a + dual_block(i, extra[i], step, first)
-
-        return lax.fori_loop(0, 3, special, sq)
+        return sq + dual_block(1, extra[1], step, first)
 
     lane_low = lane < LANES // 2
 
@@ -382,10 +405,10 @@
 
         terms = dot_nt(ys[1], lw[...].reshape(nl * bs, bs), precision=HIGHEST)
         for k in range(nr):
-            q = lax.rem(me_r + k, nr)
+            q = around(me_r, k, nr)
             total = jnp.zeros((hours, LANES), F32)
             for j in range(nl):
-                on = jnp.where(src_s[me_r * nl + j] == q, 1.0, 0.0).astype(F32)
+                on = jnp.where(src_s[j, me_r] == q, 1.0, 0.0).astype(F32)
                 total = total + on * terms[:, j * bs : (j + 1) * bs]
             pbuf[r, k] = total
         region_send(
@@ -402,13 +425,13 @@
             seg[n] = total
             return total
 
-        lax.fori_loop(0, pairs, pair, jnp.zeros((hours, LANES), F32))
+        unrolled(0, pairs, 15, pair, jnp.zeros((hours, LANES), F32))
 
         def gradient(c, _):
             grad[c] = unit_v[c] - table_s[4, c].astype(F32) * seg[table_s[3, c]]
             return 0
 
-        lax.fori_loop(0, cb, gradient, 0)
+        unrolled(0, cb, 5, gradient, 0)
         nb_src[4 + r] = grad[0, hours - 1 : hours, :]
         to_next(4 + r, r, 1)
 
@@ -467,7 +490,7 @@
             return bar, a + fold(sq)
 
         bar0, sq_p = primal(0, zero8)
-        sq_p = lax.fori_loop(1, cb, lambda c, a: primal(c, a)[1], sq_p)
+        sq_p = unrolled(1, cb, 6, lambda c, a: primal(c, a)[1], sq_p)
         new_cap = jnp.maximum(cap - primal_step * (build - capacity_grad), 0.0)
         cap_diff = new_cap - cap
         prev_new = jnp.maximum(prev_x - primal_step * prev_grad, 0.0)
@@ -497,20 +520,13 @@
     carry = lax.fori_loop(1, ITERS, later, carry)
     cap_out[...] = carry[1]
 
-    def write(c, _):
-        xst[pl.ds(c, hours, stride=cb), :] = xs[c]
-        dst[pl.ds(c, hours, stride=cb), :] = ys[c]
-        return 0
-
-    lax.fori_loop(0, cb, write, 0)
-    ox = pltpu.make_async_copy(xst, x_out, out_sem.at[0])
-    oy = pltpu.make_async_copy(dst, y_out, out_sem.at[1])
+    ox = pltpu.make_async_copy(xs, x_out, out_sem.at[0])
+    oy = pltpu.make_async_copy(ys, y_out, out_sem.at[1])
     ox.start()
     oy.start()
 
     for r in range(ITERS):
-        for k in range(nt - 1):
-            pltpu.make_async_copy(mt.at[r], mt.at[r], send_t.at[r]).wait()
+        pltpu.make_async_copy(tbuf.at[r], tbuf.at[r], send_t.at[r]).wait()
     pltpu.make_async_copy(
         gat0.at[pl.ds(0, nr - 1)], gat0.at[pl.ds(0, nr - 1)], send_g.at[0]
     ).wait()
@@ -524,6 +540,27 @@
         pltpu.make_async_copy(nb_src.at[n], nb_src.at[n], send_n.at[n]).wait()
     ox.wait()
     oy.wait()
+
+
+def by_hour(x, y):
+    cb, hours, bs = x.shape
+    some = min(16, hours)
+
+    def place(x_ref, y_ref, x_out, y_out):
+        for c in range(cb):
+            x_out[pl.ds(c, some, stride=cb), :] = x_ref[c]
+            y_out[pl.ds(c, some, stride=cb), :] = y_ref[c]
+
+    block = pl.BlockSpec((cb, some, bs), lambda i: (0, i, 0))
+    out = pl.BlockSpec((some * cb, bs), lambda i: (i, 0))
+    shape = jax.ShapeDtypeStruct((hours * cb, bs), F32)
+    return pl.pallas_call(
+        place,
+        grid=(hours // some,),
+        in_specs=[block, block],
+        out_specs=(out, out),
+        out_shape=(shape, shape),
+    )(x, y)
 
 
 def body(
@@ -555,8 +592,8 @@
     x_new, y_new, cap = pl.pallas_call(
         functools.partial(kernel, sizes),
         out_shape=(
-            jax.ShapeDtypeStruct((hours * cb, bs), F32),
-            jax.ShapeDtypeStruct((hours * cb, bs), F32),
+            jax.ShapeDtypeStruct((cb, hours, bs), F32),
+            jax.ShapeDtypeStruct((cb, hours, bs), F32),
             jax.ShapeDtypeStruct((1, LANES), F32),
         ),
         in_specs=[smem] * 4 + [vmem] * 2 + [hbm] * 4,
@@ -608,8 +645,8 @@
         ],
         compiler_params=pltpu.CompilerParams(collective_id=0, has_side_effects=True),
     )(
-        net_columns.reshape(pairs),
-        line_source.reshape(-1),
+        jnp.transpose(net_columns, (2, 0, 1)),
+        jnp.transpose(line_source),
         start_capacity,
         build_cost,
         generator_map,
@@ -620,6 +657,7 @@
         line_weights.reshape(nl * bs, bs),
     )
     own = start_capacity.shape[1]
+    x_new, y_new = by_hour(x_new, y_new)
     capacity = lax.dynamic_slice_in_dim(cap, lax.axis_index("tm") * own, own, 1)
     return (
         x_new.reshape(hours, 1, width),

time: 105 us -> 63.2 us (0.60)
  Pallas kernels: 95.7 us -> 61.1 us
  local copies, waits for them, and re-layouts: 8.22 us -> 1.21 us
    pallas_call x1, Pallas kernels: 95.7 us -> 57.4 us  [body(): pl.pallas_call(functools.partial(kernel, sizes), out_shape=(jax.ShapeDtyp...]
    unnamed x4 -> x0, local copies, waits for them, and re-layouts: 5.74 us -> none
    pallas_call x0 -> x1, Pallas kernels: none -> 3.65 us  [by_hour(): pl.pallas_call(place, grid=(hours // some,), in_specs=[block, block], out...]
    reshape x2 -> x0, local copies, waits for them, and re-layouts: 1.2 us -> none  [the longest x1 0.61 us: body(): net_columns.reshape(pairs)]
where the time goes in v2:
time: 63.2 us; the launch traced here: 62.9 us
  Pallas kernels  61.1 us (97%)
  local copies, waits for them, and re-layouts  1.21 us (2%)
  between operations  0.65 us (1%)
    pallas_call x1, Pallas kernels, body(): pl.pallas_call(functools.partial(kernel, sizes), out_shape=(jax.ShapeDtyp...  57.4 us
    pallas_call x1, Pallas kernels, by_hour(): pl.pallas_call(place, grid=(hours // some,), in_specs=[block, block], out...  3.65 us

profile of v2, /device:TPU:1, one launch (start us, length us, event | category | flops | bytes accessed | tf_op | source)
XLA Modules:
  0.0 62.9 jit_solution(6948879238441034687)
XLA Ops:
  0.6 57.4 %shard_map.121 = (f32[25,64,128]{2,1,0:T(8,128)}, f32[25,64,128]{2,1,0:T(8,128)}, f32[1,128]{1,0:T(1,128)}) custom-call(s32[3,1,25]{2,1,0:T(1,128)} %bitcast.15, s32[4,8]{1,0:T(4,128)} %bitcast.14, f32[1,4]{1,0:T(1,128)} %cap_s.1, f32[1,4]{1,0:T(1,128)} %build_s.1, s32[1,128]{1,0:T(1,128)} %gm_v.1, f32[25,1,128]{2,1,0:T(1,128)} %bitcast.13, ...), custom_call_target="tpu_custom_call" | custom-call | tf_op jit(solution)/shard_map/pallas_call | solution.py:592
  58.1 1.2 %constant_dynamic-slice_fusion = f32[1,4]{1,0:T(1,128)} fusion(f32[1,128]{1,0:T(1,128)} %get-tuple-element.12, s32[]{:T(128)S(6)} %select_n.3), kind=kLoop, calls=%fused_computation | loop fusion | bytes 36 | tf_op jit(solution)/shard_map/dynamic_slice | solution.py:661
  59.3 3.7 %shard_map.122 = (f32[1600,128]{1,0:T(8,128)}, f32[1600,128]{1,0:T(8,128)}) custom-call(f32[25,64,128]{2,1,0:T(8,128)} %get-tuple-element.8.x_ref, f32[25,64,128]{2,1,0:T(8,128)} %get-tuple-element.9.y_ref), custom_call_target="tpu_custom_call" | custom-call | tf_op jit(solution)/shard_map/pallas_call | solution.py:557

commit v3 on v2

--- a/solution.py
+++ b/solution.py
@@ -54,17 +54,18 @@
     dem_hbm,
     w_hbm,
     lw_hbm,
-    x_out,
-    y_out,
+    xs,
+    ys,
     cap_out,
     xst,
     dst,
     wst,
     lw,
+    lwh,
+    lwl,
     wh,
     wl,
-    xs,
-    ys,
+    tgt,
     grad,
     xb,
     yb,
@@ -89,7 +90,6 @@
     nb_dst,
     load_sem,
     w_sem,
-    out_sem,
     send_t,
     recv_t,
     send_r,
@@ -124,12 +124,21 @@
         at = me + k
         return jnp.where(at >= count, at - count, at)
 
-    @pl.loop(0, nt - 1)
-    def _(step):
-        k = offset_of(step, nt)
-        pl.semaphore_signal(
-            barrier, inc=1, device_id=(around(me_t, k, nt), me_r), device_id_type=MESH
-        )
+    nx = 4 if nt % 4 == 0 else 1
+    nz = nt // nx
+    me_z, me_x = me_t // nx, me_t % nx
+
+    def tm_partners(act):
+        order = [(dz, dx) for dz in range(nz) for dx in range(nx) if dz or dx]
+        order.sort(key=lambda d: -min(d[0], nz - d[0]) - min(d[1], nx - d[1]))
+        for dz, dx in order:
+            act(dz * nx + dx - 1, around(me_z, dz, nz) * nx + around(me_x, dx, nx))
+
+    tm_partners(
+        lambda slot, at: pl.semaphore_signal(
+            barrier, inc=1, device_id=(at, me_r), device_id_type=MESH
+        )
+    )
 
     @pl.loop(0, nr - 1)
     def _(step):
@@ -217,20 +226,32 @@
     for i in range(cb // 2):
         split_weights(i)
 
+    cd.wait()
+    cl.wait()
+
+    def place_target(i, _):
+        tgt[i] = dst[pl.ds(i, hours, stride=cb), :]
+        return 0
+
+    unrolled(0, cb, 5, place_target, 0)
+    line_high = lw[...].astype(BF16)
+    lwh[...] = line_high
+    lwl[...] = (lw[...] - line_high.astype(F32)).astype(BF16)
+
     pl.semaphore_wait(barrier, nt - 1 + nr - 1)
 
     def tm_send(r):
-        @pl.loop(0, nt - 1)
-        def _(step):
-            k = offset_of(step, nt)
+        def send(slot, at):
             pltpu.make_async_remote_copy(
                 src_ref=mt.at[r],
-                dst_ref=tbuf.at[r, k - 1],
+                dst_ref=tbuf.at[r, slot],
                 send_sem=send_t.at[r],
                 recv_sem=recv_t.at[r],
-                device_id=(around(me_t, k, nt), me_r),
+                device_id=(at, me_r),
                 device_id_type=MESH,
             ).start()
+
+        tm_partners(send)
 
     def tm_sum(r):
         pltpu.make_async_copy(tbuf.at[r], tbuf.at[r], recv_t.at[r]).wait()
@@ -307,9 +328,9 @@
         last = jnp.dot(x3[0:hours], low, preferred_element_type=F32)
         return both[0:hours] + both[hours:] + last
 
-    def dual_block(i, target, step, first):
+    def dual_block(i, rest, step, first):
         low = jnp.where(i < 3, LOW, 0.0)
-        move = step * (target - network(i))
+        move = step * rest
         if first:
             new = jnp.maximum(move, low)
             change = new
@@ -326,31 +347,37 @@
 
     def line_apply(block_of):
         parts = jnp.concatenate([block_of(src_s[j, me_r]) for j in range(nl)], axis=1)
-        return jnp.dot(parts, lw[...], precision=HIGHEST, preferred_element_type=F32)
+        high = parts.astype(BF16)
+        low = (parts - high.astype(F32)).astype(BF16)
+        return (
+            jnp.dot(high, lwh[...], preferred_element_type=F32)
+            + jnp.dot(low, lwh[...], preferred_element_type=F32)
+            + jnp.dot(high, lwl[...], preferred_element_type=F32)
+        )
 
     row = lax.broadcasted_iota(jnp.int32, (hours, LANES), 0)
     has_before = jnp.where(me_t > 0, 1.0, 0.0).astype(F32)
     has_after = jnp.where(me_t < nt - 1, 1.0, 0.0).astype(F32)
 
     def forward(bar0, prev_bar, cap_bar, line_flow, step, first):
-        def plain(i, a):
-            return a + dual_block(i, target_of(i), step, first)
-
-        sq = unrolled(3, cb, 11, plain, zero8)
         earlier = pltpu.roll(bar0, 1, 0)
         earlier = jnp.where(row == 0, prev_bar * has_before, earlier)
-        extra[0] = target_of(0) + earlier
+        tgt[0] = target_of(0) + earlier
         picked = jnp.dot(
             jnp.broadcast_to(cap_bar(), (8, LANES)),
             sel_t,
             precision=HIGHEST,
             preferred_element_type=F32,
         )[0:1]
-        extra[2] = target_of(2) - couple * picked
-        sq = sq + dual_block(0, extra[0], step, first)
-        sq = sq + dual_block(2, extra[2], step, first)
-        extra[1] = target_of(1) - line_flow()
-        return sq + dual_block(1, extra[1], step, first)
+        tgt[2] = target_of(2) - couple * picked
+        tgt[1] = target_of(1) - network(1)
+
+        def plain(n, a):
+            i = jnp.where(n > 0, n + 1, 0)
+            return a + dual_block(i, tgt[i] - network(i), step, first)
+
+        sq = unrolled(0, cb - 1, 12, plain, zero8)
+        return sq + dual_block(1, tgt[1] - line_flow(), step, first)
 
     lane_low = lane < LANES // 2
 
@@ -361,8 +388,6 @@
         d = d + pltpu.roll(d, LANES // 2, 1)
         return jnp.where(lane_low, p, d)
 
-    cl.wait()
-    cd.wait()
     gathered = []
 
     def first_capacity():
@@ -403,7 +428,12 @@
         tm_send(it)
         to_next(1 + r, r, -1)
 
-        terms = dot_nt(ys[1], lw[...].reshape(nl * bs, bs), precision=HIGHEST)
+        y1 = yb[1]
+        terms = (
+            dot_nt(y1[0:hours], lwh[...])
+            + dot_nt(y1[hours:], lwh[...])
+            + dot_nt(y1[0:hours], lwl[...])
+        )
         for k in range(nr):
             q = around(me_r, k, nr)
             total = jnp.zeros((hours, LANES), F32)
@@ -518,12 +548,7 @@
         sq_d,
     )
     carry = lax.fori_loop(1, ITERS, later, carry)
-    cap_out[...] = carry[1]
-
-    ox = pltpu.make_async_copy(xs, x_out, out_sem.at[0])
-    oy = pltpu.make_async_copy(ys, y_out, out_sem.at[1])
-    ox.start()
-    oy.start()
+    cap_out[...] = pltpu.roll(carry[1], lax.rem(LANES - me_t * own_n, LANES), 1)
 
     for r in range(ITERS):
         pltpu.make_async_copy(tbuf.at[r], tbuf.at[r], send_t.at[r]).wait()
@@ -538,29 +563,38 @@
         ).wait()
     for n in range(1 + 2 * (ITERS - 1)):
         pltpu.make_async_copy(nb_src.at[n], nb_src.at[n], send_n.at[n]).wait()
-    ox.wait()
-    oy.wait()
-
-
-def by_hour(x, y):
-    cb, hours, bs = x.shape
-    some = min(16, hours)
-
-    def place(x_ref, y_ref, x_out, y_out):
+
+
+def by_hour(x, y, cap, own):
+    cb, hours, _, bs = x.shape
+
+    def place(x_ref, y_ref, cap_ref, x_out, y_out, cap_out, sem):
+        copies = []
         for c in range(cb):
-            x_out[pl.ds(c, some, stride=cb), :] = x_ref[c]
-            y_out[pl.ds(c, some, stride=cb), :] = y_ref[c]
-
-    block = pl.BlockSpec((cb, some, bs), lambda i: (0, i, 0))
-    out = pl.BlockSpec((some * cb, bs), lambda i: (i, 0))
-    shape = jax.ShapeDtypeStruct((hours * cb, bs), F32)
+            at = pl.ds(c * bs, bs)
+            copies.append(pltpu.make_async_copy(x_ref.at[c], x_out.at[:, :, at], sem.at[0, c]))
+            copies.append(pltpu.make_async_copy(y_ref.at[c], y_out.at[:, :, at], sem.at[1, c]))
+        for copy in copies:
+            copy.start()
+        cap_out[...] = cap_ref[:, 0:own]
+        for copy in copies:
+            copy.wait()
+
+    vmem = pl.BlockSpec(memory_space=pltpu.VMEM)
+    hbm = pl.BlockSpec(memory_space=pl.ANY)
+    shape = jax.ShapeDtypeStruct((hours, 1, cb * bs), F32)
     return pl.pallas_call(
         place,
-        grid=(hours // some,),
-        in_specs=[block, block],
-        out_specs=(out, out),
-        out_shape=(shape, shape),
-    )(x, y)
+        in_specs=[vmem, vmem, vmem],
+        out_specs=(hbm, hbm, vmem),
+        out_shape=(shape, shape, jax.ShapeDtypeStruct((1, own), F32)),
+        scratch_shapes=[pltpu.SemaphoreType.DMA((2, cb))],
+        compiler_params=pltpu.CompilerParams(vmem_limit_bytes=8 * 2**20),
+    )(x, y, cap)
+
+
+def in_hbm(value):
+    return pltpu.with_memory_space_constraint(value, pltpu.HBM)
 
 
 def body(
@@ -586,7 +620,7 @@
     sizes = (hours, cb, bs, s_count, nl, nt, nr)
     smem = pl.BlockSpec(memory_space=pltpu.SMEM)
     vmem = pl.BlockSpec(memory_space=pltpu.VMEM)
-    hbm = pl.BlockSpec(memory_space=pl.ANY)
+    hbm = pl.BlockSpec(memory_space=pltpu.HBM)
     rounds = ITERS - 1
     dma = pltpu.SemaphoreType.DMA
     x_new, y_new, cap = pl.pallas_call(
@@ -597,15 +631,16 @@
             jax.ShapeDtypeStruct((1, LANES), F32),
         ),
         in_specs=[smem] * 4 + [vmem] * 2 + [hbm] * 4,
-        out_specs=(hbm, hbm, vmem),
+        out_specs=(vmem, vmem, vmem),
         scratch_shapes=[
             pltpu.VMEM((hours * cb, bs), F32),
             pltpu.VMEM((hours * cb, bs), F32),
             pltpu.VMEM((cb, s_count, bs, bs), F32),
             pltpu.VMEM((nl * bs, bs), F32),
+            pltpu.VMEM((nl * bs, bs), BF16),
+            pltpu.VMEM((nl * bs, bs), BF16),
             pltpu.VMEM((pairs, bs, bs), BF16),
             pltpu.VMEM((pairs, bs, bs), BF16),
-            pltpu.VMEM((cb, hours, bs), F32),
             pltpu.VMEM((cb, hours, bs), F32),
             pltpu.VMEM((cb, hours, bs), F32),
             pltpu.VMEM((cb, 2 * hours, bs), BF16),
@@ -631,7 +666,6 @@
             pltpu.VMEM((1 + 2 * rounds, 1, LANES), F32),
             dma((5,)),
             dma((cb,)),
-            dma((2,)),
             dma((ITERS,)),
             dma((ITERS,)),
             dma((rounds,)),
@@ -643,8 +677,10 @@
             dma((1 + 2 * rounds,)),
             dma((1 + 2 * rounds,)),
         ],
-        compiler_params=pltpu.CompilerParams(collective_id=0, has_side_effects=True),
-    )(
+        compiler_params=pltpu.CompilerParams(
+            collective_id=0, has_side_effects=True, vmem_limit_bytes=40 * 2**20
+        ),
+    )(*(in_hbm(v) for v in (
         jnp.transpose(net_columns, (2, 0, 1)),
         jnp.transpose(line_source),
         start_capacity,
@@ -655,15 +691,9 @@
         demand.reshape(hours * cb, bs),
         net_weights[0],
         line_weights.reshape(nl * bs, bs),
-    )
-    own = start_capacity.shape[1]
-    x_new, y_new = by_hour(x_new, y_new)
-    capacity = lax.dynamic_slice_in_dim(cap, lax.axis_index("tm") * own, own, 1)
-    return (
-        x_new.reshape(hours, 1, width),
-        y_new.reshape(hours, 1, width),
-        capacity,
-    )
+    )))
+    parts = (cb, hours, 1, bs)
+    return by_hour(x_new.reshape(parts), y_new.reshape(parts), cap, start_capacity.shape[1])
 
 
 def solution(mesh):

time: 63.2 us -> 58.8 us (0.930)
  Pallas kernels: 61.1 us -> 58 us
  local copies, waits for them, and re-layouts: 1.21 us -> 0 us
    pallas_call x1, Pallas kernels: 3.65 us -> 2.09 us  [by_hour(): pl.pallas_call(place, in_specs=[vmem, vmem, vmem], out_specs=(hbm, hbm, v...]
    pallas_call x1, Pallas kernels: 57.4 us -> 55.9 us  [body(): pl.pallas_call(functools.partial(kernel, sizes), out_shape=(jax.ShapeDtyp...]
    dynamic_slice x1 -> x0, local copies, waits for them, and re-layouts: 1.21 us -> none  [body(): capacity = lax.dynamic_slice_in_dim(cap, lax.axis_index('tm') * own, own, 1)]
where the time goes in v3:
time: 58.8 us; the launch traced here: 58.7 us
  Pallas kernels  58 us (99%)
  between operations  0.64 us (1%)
    pallas_call x1, Pallas kernels, body(): pl.pallas_call(functools.partial(kernel, sizes), out_shape=(jax.ShapeDtyp...  55.9 us
    pallas_call x1, Pallas kernels, by_hour(): pl.pallas_call(place, in_specs=[vmem, vmem, vmem], out_specs=(hbm, hbm, v...  2.09 us

profile of v3, /device:TPU:1, one launch (start us, length us, event | category | flops | bytes accessed | tf_op | source)
XLA Modules:
  0.0 58.7 jit_solution(2173801049421321509)
XLA Ops:
  0.6 55.9 %shard_map.121 = (f32[25,64,128]{2,1,0:T(8,128)S(1)}, f32[25,64,128]{2,1,0:T(8,128)S(1)}, f32[1,128]{1,0:T(1,128)S(1)}) custom-call(s32[3,1,25]{2,1,0:T(1,128)} %bitcast.17, s32[4,8]{1,0:T(4,128)} %bitcast.16, f32[1,4]{1,0:T(1,128)} %cap_s.1, f32[1,4]{1,0:T(1,128)} %build_s.1, s32[1,128]{1,0:T(1,128)} %gm_v.1, f32[25,1,128]{2,1,0:T(1,128)} %bitcast.15, ...), custom_call_target="tpu_custom_call" | custom-call | tf_op jit(solution)/shard_map/pallas_call | solution.py:626
  56.6 2.1 %shard_map.122 = (f32[64,1,3200]{2,1,0:T(1,128)}, f32[64,1,3200]{2,1,0:T(1,128)}, f32[1,4]{1,0:T(1,128)}) custom-call(f32[25,64,1,128]{3,2,1,0:T(1,128)S(1)} %bitcast.9, f32[25,64,1,128]{3,2,1,0:T(1,128)S(1)} %bitcast.10, f32[1,128]{1,0:T(1,128)S(1)} %get-tuple-element.8.cap_ref), custom_call_target="tpu_custom_call" | custom-call | tf_op jit(solution)/shard_map/pallas_call | solution.py:586

commit v4 on v3

--- a/solution.py
+++ b/solution.py
@@ -44,12 +44,12 @@
 
 def kernel(
     sizes,
-    cols_s,
-    src_s,
-    cap_s,
-    build_s,
-    gm_v,
-    unit_v,
+    cols_hbm,
+    src_hbm,
+    cap_hbm,
+    build_hbm,
+    gm_hbm,
+    unit_hbm,
     x_hbm,
     dem_hbm,
     w_hbm,
@@ -57,6 +57,12 @@
     xs,
     ys,
     cap_out,
+    cols_s,
+    src_s,
+    cap_s,
+    build_s,
+    gm_v,
+    unit_v,
     xst,
     dst,
     wst,
@@ -110,9 +116,16 @@
     couple = 1.0 / math.sqrt(hours * nt)
 
     cx = pltpu.make_async_copy(x_hbm, xst, load_sem.at[0])
+    cu = pltpu.make_async_copy(unit_hbm, unit_v, load_sem.at[5])
+    cc = pltpu.make_async_copy(cap_hbm, cap_s, load_sem.at[6])
+    cbuild = pltpu.make_async_copy(build_hbm, build_s, load_sem.at[7])
+    ck = pltpu.make_async_copy(cols_hbm, cols_s, load_sem.at[8])
+    cs = pltpu.make_async_copy(src_hbm, src_s, load_sem.at[9])
+    cg = pltpu.make_async_copy(gm_hbm, gm_v, load_sem.at[10])
     cd = pltpu.make_async_copy(dem_hbm, dst, load_sem.at[1])
     cl = pltpu.make_async_copy(lw_hbm, lw, load_sem.at[2])
-    cx.start()
+    for c in (cx, cu, cc, cbuild):
+        c.start()
 
     barrier = pltpu.get_barrier_semaphore()
 
@@ -147,8 +160,8 @@
             barrier, inc=1, device_id=(me_t, around(me_r, k, nr)), device_id_type=MESH
         )
 
-    cd.start()
-    cl.start()
+    for c in (ck, cs, cg, cd, cl):
+        c.start()
     w_copies = [
         pltpu.make_async_copy(w_hbm.at[i], wst.at[i], w_sem.at[i]) for i in range(cb)
     ]
@@ -156,6 +169,84 @@
         c.start()
 
     lane = lax.broadcasted_iota(jnp.int32, (1, LANES), 1)
+
+    own_n = LANES // nt
+    cc.wait()
+    cbuild.wait()
+    cap_vec = jnp.zeros((1, LANES), F32)
+    build_vec = jnp.zeros((1, LANES), F32)
+    for k in range(own_n):
+        here = lane == me_t * own_n + k
+        cap_vec = jnp.where(here, cap_s[0, k], cap_vec)
+        build_vec = jnp.where(here, build_s[0, k], build_vec)
+    mt[0, :, 0:LANES] = cap_vec
+    mt[0, :, LANES : 2 * LANES] = build_vec
+
+    cx.wait()
+    cu.wait()
+    vx[0:hours, :] = xst[pl.ds(3, hours, stride=cb), :]
+    vx[hours : hours + 8, :] = jnp.broadcast_to(unit_v[3], (8, LANES))
+    nb_src[0] = xst[pl.ds((hours - 1) * cb, 1), :]
+
+    pl.semaphore_wait(barrier, nt - 1 + nr - 1)
+
+    def tm_send(r):
+        def send(slot, at):
+            pltpu.make_async_remote_copy(
+                src_ref=mt.at[r],
+                dst_ref=tbuf.at[r, slot],
+                send_sem=send_t.at[r],
+                recv_sem=recv_t.at[r],
+                device_id=(at, me_r),
+                device_id_type=MESH,
+            ).start()
+
+        tm_partners(send)
+
+    def tm_sum(r):
+        pltpu.make_async_copy(tbuf.at[r], tbuf.at[r], recv_t.at[r]).wait()
+        total = mt[r]
+        for k in range(nt - 1):
+            total = total + tbuf[r, k]
+        return total
+
+    def region_send(src, dst_of, send_sem, recv_sem):
+        @pl.loop(0, nr - 1)
+        def _(step):
+            k = offset_of(step, nr)
+            pltpu.make_async_remote_copy(
+                src_ref=src(k),
+                dst_ref=dst_of(k),
+                send_sem=send_sem,
+                recv_sem=recv_sem,
+                device_id=(me_t, around(me_r, k, nr)),
+                device_id_type=MESH,
+            ).start()
+
+    def to_next(n, r, by):
+        pltpu.make_async_remote_copy(
+            src_ref=nb_src.at[n],
+            dst_ref=nb_dst.at[n],
+            send_sem=send_n.at[n],
+            recv_sem=recv_n.at[n],
+            device_id=(around(me_t, (by + nt) % nt, nt), me_r),
+            device_id_type=MESH,
+        ).start()
+
+    def next_wait(n):
+        pltpu.make_async_copy(nb_dst.at[n], nb_dst.at[n], recv_n.at[n]).wait()
+
+    tm_send(0)
+    region_send(
+        lambda k: vx, lambda k: gat0.at[me_r], send_g.at[0], recv_g.at[0]
+    )
+    to_next(0, 0, 1)
+    gat0[me_r] = vx[...]
+
+    ck.wait()
+    cs.wait()
+    cg.wait()
+
 
     def column(p):
         return cols_s[p % s_count, 0, p // s_count]
@@ -174,21 +265,6 @@
     rank_v[...] = rank
     c1 = pltpu.make_async_copy(rank_v, rank_s, load_sem.at[3])
     c1.start()
-
-    own_n = LANES // nt
-    cap_vec = jnp.zeros((1, LANES), F32)
-    build_vec = jnp.zeros((1, LANES), F32)
-    for k in range(own_n):
-        here = lane == me_t * own_n + k
-        cap_vec = jnp.where(here, cap_s[0, k], cap_vec)
-        build_vec = jnp.where(here, build_s[0, k], build_vec)
-    mt[0, :, 0:LANES] = cap_vec
-    mt[0, :, LANES : 2 * LANES] = build_vec
-
-    cx.wait()
-    vx[0:hours, :] = xst[pl.ds(3, hours, stride=cb), :]
-    vx[hours : hours + 8, :] = jnp.broadcast_to(unit_v[3], (8, LANES))
-    nb_src[0] = xst[pl.ds((hours - 1) * cb, 1), :]
 
     sel_t = jnp.where(
         gm_v[...] == lax.broadcasted_iota(jnp.int32, (LANES, LANES), 0), 1.0, 0.0
@@ -223,7 +299,7 @@
             wh[i * s_count + s] = high
             wl[i * s_count + s] = (w - high.astype(F32)).astype(BF16)
 
-    for i in range(cb // 2):
+    for i in range(cb):
         split_weights(i)
 
     cd.wait()
@@ -237,61 +313,6 @@
     line_high = lw[...].astype(BF16)
     lwh[...] = line_high
     lwl[...] = (lw[...] - line_high.astype(F32)).astype(BF16)
-
-    pl.semaphore_wait(barrier, nt - 1 + nr - 1)
-
-    def tm_send(r):
-        def send(slot, at):
-            pltpu.make_async_remote_copy(
-                src_ref=mt.at[r],
-                dst_ref=tbuf.at[r, slot],
-                send_sem=send_t.at[r],
-                recv_sem=recv_t.at[r],
-                device_id=(at, me_r),
-                device_id_type=MESH,
-            ).start()
-
-        tm_partners(send)
-
-    def tm_sum(r):
-        pltpu.make_async_copy(tbuf.at[r], tbuf.at[r], recv_t.at[r]).wait()
-        total = mt[r]
-        for k in range(nt - 1):
-            total = total + tbuf[r, k]
-        return total
-
-    def region_send(src, dst_of, send_sem, recv_sem):
-        @pl.loop(0, nr - 1)
-        def _(step):
-            k = offset_of(step, nr)
-            pltpu.make_async_remote_copy(
-                src_ref=src(k),
-                dst_ref=dst_of(k),
-                send_sem=send_sem,
-                recv_sem=recv_sem,
-                device_id=(me_t, around(me_r, k, nr)),
-                device_id_type=MESH,
-            ).start()
-
-    def to_next(n, r, by):
-        pltpu.make_async_remote_copy(
-            src_ref=nb_src.at[n],
-            dst_ref=nb_dst.at[n],
-            send_sem=send_n.at[n],
-            recv_sem=recv_n.at[n],
-            device_id=(around(me_t, (by + nt) % nt, nt), me_r),
-            device_id_type=MESH,
-        ).start()
-
-    def next_wait(n):
-        pltpu.make_async_copy(nb_dst.at[n], nb_dst.at[n], recv_n.at[n]).wait()
-
-    region_send(
-        lambda k: vx, lambda k: gat0.at[me_r], send_g.at[0], recv_g.at[0]
-    )
-    tm_send(0)
-    to_next(0, 0, 1)
-    gat0[me_r] = vx[...]
 
     def primal_block(c, x, g, step):
         low = jnp.where(c == 3, LOW, 0.0)
@@ -304,9 +325,6 @@
 
     def fold(sq):
         return jnp.sum(sq.reshape(hours // 8, 8, LANES), axis=0)
-
-    for i in range(cb // 2, cb):
-        split_weights(i)
 
     first_step = STEP_SCALE
 
@@ -618,7 +636,6 @@
     nr = lax.axis_size("region")
     pairs = cb * s_count
     sizes = (hours, cb, bs, s_count, nl, nt, nr)
-    smem = pl.BlockSpec(memory_space=pltpu.SMEM)
     vmem = pl.BlockSpec(memory_space=pltpu.VMEM)
     hbm = pl.BlockSpec(memory_space=pltpu.HBM)
     rounds = ITERS - 1
@@ -630,9 +647,15 @@
             jax.ShapeDtypeStruct((cb, hours, bs), F32),
             jax.ShapeDtypeStruct((1, LANES), F32),
         ),
-        in_specs=[smem] * 4 + [vmem] * 2 + [hbm] * 4,
+        in_specs=[hbm] * 10,
         out_specs=(vmem, vmem, vmem),
         scratch_shapes=[
+            pltpu.SMEM((s_count, 1, cb), jnp.int32),
+            pltpu.SMEM(line_source.shape[::-1], jnp.int32),
+            pltpu.SMEM(start_capacity.shape, F32),
+            pltpu.SMEM(build_cost.shape, F32),
+            pltpu.VMEM(generator_map.shape, jnp.int32),
+            pltpu.VMEM((cb, 1, bs), F32),
             pltpu.VMEM((hours * cb, bs), F32),
             pltpu.VMEM((hours * cb, bs), F32),
             pltpu.VMEM((cb, s_count, bs, bs), F32),
@@ -664,7 +687,7 @@
             pltpu.VMEM((rounds, nr - 1, 1, LANES), F32),
             pltpu.VMEM((1 + 2 * rounds, 1, LANES), F32),
             pltpu.VMEM((1 + 2 * rounds, 1, LANES), F32),
-            dma((5,)),
+            dma((11,)),
             dma((cb,)),
             dma((ITERS,)),
             dma((ITERS,)),

time: 58.8 us -> 58.1 us (0.988)
  Pallas kernels: 58 us -> 57.4 us
    pallas_call x1, Pallas kernels: 55.9 us -> 55.3 us  [body(): pl.pallas_call(functools.partial(kernel, sizes), out_shape=(jax.ShapeDtyp...]
where the time goes in v4:
time: 58.1 us; the launch traced here: 58 us
  Pallas kernels  57.4 us (99%)
  between operations  0.64 us (1%)
    pallas_call x1, Pallas kernels, body(): pl.pallas_call(functools.partial(kernel, sizes), out_shape=(jax.ShapeDtyp...  55.3 us
    pallas_call x1, Pallas kernels, by_hour(): pl.pallas_call(place, in_specs=[vmem, vmem, vmem], out_specs=(hbm, hbm, v...  2.09 us

profile of v4, /device:TPU:1, one launch (start us, length us, event | category | flops | bytes accessed | tf_op | source)
XLA Modules:
  0.0 58.0 jit_solution(2638354654522536232)
XLA Ops:
  0.6 55.3 %shard_map.121 = (f32[25,64,128]{2,1,0:T(8,128)S(1)}, f32[25,64,128]{2,1,0:T(8,128)S(1)}, f32[1,128]{1,0:T(1,128)S(1)}) custom-call(s32[3,1,25]{2,1,0:T(1,128)} %bitcast.17, s32[4,8]{1,0:T(4,128)} %bitcast.16, f32[1,4]{1,0:T(1,128)} %cap_hbm.1, f32[1,4]{1,0:T(1,128)} %build_hbm.1, s32[1,128]{1,0:T(1,128)} %gm_hbm.1, f32[25,1,128]{2,1,0:T(1,128)} %bitcast.15, ...), custom_call_target="tpu_custom_call" | custom-call | tf_op jit(solution)/shard_map/pallas_call | solution.py:643
  56.0 2.1 %shard_map.122 = (f32[64,1,3200]{2,1,0:T(1,128)}, f32[64,1,3200]{2,1,0:T(1,128)}, f32[1,4]{1,0:T(1,128)}) custom-call(f32[25,64,1,128]{3,2,1,0:T(1,128)S(1)} %bitcast.9, f32[25,64,1,128]{3,2,1,0:T(1,128)S(1)} %bitcast.10, f32[1,128]{1,0:T(1,128)S(1)} %get-tuple-element.8.cap_ref), custom_call_target="tpu_custom_call" | custom-call | tf_op jit(solution)/shard_map/pallas_call | solution.py:604

commit v5 on v4

--- a/solution.py
+++ b/solution.py
@@ -205,10 +205,10 @@
 
     def tm_sum(r):
         pltpu.make_async_copy(tbuf.at[r], tbuf.at[r], recv_t.at[r]).wait()
-        total = mt[r]
-        for k in range(nt - 1):
-            total = total + tbuf[r, k]
-        return total
+        parts = [mt[r]] + [tbuf[r, k] for k in range(nt - 1)]
+        while len(parts) > 1:
+            parts = [sum(parts[n + 1 : n + 2], parts[n]) for n in range(0, len(parts), 2)]
+        return parts[0]
 
     def region_send(src, dst_of, send_sem, recv_sem):
         @pl.loop(0, nr - 1)
@@ -380,22 +380,32 @@
     def forward(bar0, prev_bar, cap_bar, line_flow, step, first):
         earlier = pltpu.roll(bar0, 1, 0)
         earlier = jnp.where(row == 0, prev_bar * has_before, earlier)
-        tgt[0] = target_of(0) + earlier
-        picked = jnp.dot(
-            jnp.broadcast_to(cap_bar(), (8, LANES)),
-            sel_t,
-            precision=HIGHEST,
-            preferred_element_type=F32,
-        )[0:1]
-        tgt[2] = target_of(2) - couple * picked
-        tgt[1] = target_of(1) - network(1)
-
-        def plain(n, a):
-            i = jnp.where(n > 0, n + 1, 0)
+
+        def capacity_term():
+            return couple * jnp.dot(
+                jnp.broadcast_to(cap_bar(), (8, LANES)),
+                sel_t,
+                precision=HIGHEST,
+                preferred_element_type=F32,
+            )[0:1]
+
+        def plain(i, a):
             return a + dual_block(i, tgt[i] - network(i), step, first)
 
-        sq = unrolled(0, cb - 1, 12, plain, zero8)
-        return sq + dual_block(1, tgt[1] - line_flow(), step, first)
+        if first:
+            sq = unrolled(3, cb, 11, plain, zero8)
+        else:
+            picked = capacity_term()
+            sq = zero8
+            for i in range(3, cb):
+                sq = plain(i, sq)
+        sq = sq + dual_block(0, tgt[0] + earlier - network(0), step, first)
+        rest = tgt[2] - network(2)
+        last = tgt[1] - network(1)
+        if first:
+            picked = capacity_term()
+        sq = sq + dual_block(2, rest - picked, step, first)
+        return sq + dual_block(1, last - line_flow(), step, first)
 
     lane_low = lane < LANES // 2
 

time: 58.1 us -> 55.9 us (0.962)
  Pallas kernels: 57.4 us -> 55.1 us
    pallas_call x1, Pallas kernels: 55.3 us -> 53 us  [body(): pl.pallas_call(functools.partial(kernel, sizes), out_shape=(jax.ShapeDtyp...]
where the time goes in v5:
time: 55.9 us; the launch traced here: 55.8 us
  Pallas kernels  55.1 us (99%)
  between operations  0.64 us (1%)
    pallas_call x1, Pallas kernels, body(): pl.pallas_call(functools.partial(kernel, sizes), out_shape=(jax.ShapeDtyp...  53 us
    pallas_call x1, Pallas kernels, by_hour(): pl.pallas_call(place, in_specs=[vmem, vmem, vmem], out_specs=(hbm, hbm, v...  2.09 us

profile of v5, /device:TPU:1, one launch (start us, length us, event | category | flops | bytes accessed | tf_op | source)
XLA Modules:
  0.0 55.8 jit_solution(4613745438273969113)
XLA Ops:
  0.6 53.0 %shard_map.121 = (f32[25,64,128]{2,1,0:T(8,128)S(1)}, f32[25,64,128]{2,1,0:T(8,128)S(1)}, f32[1,128]{1,0:T(1,128)S(1)}) custom-call(s32[3,1,25]{2,1,0:T(1,128)} %bitcast.17, s32[4,8]{1,0:T(4,128)} %bitcast.16, f32[1,4]{1,0:T(1,128)} %cap_hbm.1, f32[1,4]{1,0:T(1,128)} %build_hbm.1, s32[1,128]{1,0:T(1,128)} %gm_hbm.1, f32[25,1,128]{2,1,0:T(1,128)} %bitcast.15, ...), custom_call_target="tpu_custom_call" | custom-call | tf_op jit(solution)/shard_map/pallas_call | solution.py:653
  53.7 2.1 %shard_map.122 = (f32[64,1,3200]{2,1,0:T(1,128)}, f32[64,1,3200]{2,1,0:T(1,128)}, f32[1,4]{1,0:T(1,128)}) custom-call(f32[25,64,1,128]{3,2,1,0:T(1,128)S(1)} %bitcast.9, f32[25,64,1,128]{3,2,1,0:T(1,128)S(1)} %bitcast.10, f32[1,128]{1,0:T(1,128)S(1)} %get-tuple-element.8.cap_ref), custom_call_target="tpu_custom_call" | custom-call | tf_op jit(solution)/shard_map/pallas_call | solution.py:614

commit v6 on v5

--- a/solution.py
+++ b/solution.py
@@ -127,6 +127,9 @@
     for c in (cx, cu, cc, cbuild):
         c.start()
 
+    def rows_of(c):
+        return pl.ds(c, hours, stride=cb)
+
     barrier = pltpu.get_barrier_semaphore()
 
     def offset_of(step, count):
@@ -162,9 +165,11 @@
 
     for c in (ck, cs, cg, cd, cl):
         c.start()
-    w_copies = [
-        pltpu.make_async_copy(w_hbm.at[i], wst.at[i], w_sem.at[i]) for i in range(cb)
-    ]
+    chunk = 5 if cb % 5 == 0 else 1
+    w_copies = []
+    for n in range(cb // chunk):
+        at = pl.ds(n * chunk, chunk)
+        w_copies.append(pltpu.make_async_copy(w_hbm.at[at], wst.at[at], w_sem.at[n]))
     for c in w_copies:
         c.start()
 
@@ -289,18 +294,16 @@
     c2 = pltpu.make_async_copy(table_v, table_s, load_sem.at[4])
     c2.start()
 
-    def split_weights(i):
-        w_copies[i].wait()
-
-        @pl.loop(0, s_count)
-        def _(s):
-            w = wst[i, s]
-            high = w.astype(BF16)
-            wh[i * s_count + s] = high
-            wl[i * s_count + s] = (w - high.astype(F32)).astype(BF16)
-
-    for i in range(cb):
-        split_weights(i)
+    for n, copy in enumerate(w_copies):
+        copy.wait()
+
+        @pl.loop(n * chunk, (n + 1) * chunk)
+        def _(i):
+            for s in range(s_count):
+                w = wst[i, s]
+                high = w.astype(BF16)
+                wh[i * s_count + s] = high
+                wl[i * s_count + s] = (w - high.astype(F32)).astype(BF16)
 
     cd.wait()
     cl.wait()
@@ -319,7 +322,7 @@
         new = jnp.maximum(x - step * g, low)
         change = new - x
         bar = new + change
-        xs[c] = new
+        xs[rows_of(c), :] = new
         xb[c] = split(bar)
         return bar, change * change
 
@@ -353,10 +356,10 @@
             new = jnp.maximum(move, low)
             change = new
         else:
-            old = ys[i]
+            old = ys[rows_of(i), :]
             new = jnp.maximum(old + move, low)
             change = new - old
-        ys[i] = new
+        ys[rows_of(i), :] = new
         yb[i] = split(new)
         return fold(change * change)
 
@@ -450,9 +453,9 @@
     def later(it, carry):
         prev_x, cap, cap_change, weight, sq_p, sq_d = carry
         r = it - 1
-        mt[it, :, 0:LANES] = jnp.sum(ys[2], axis=0, keepdims=True)
+        mt[it, :, 0:LANES] = jnp.sum(ys[rows_of(2), :], axis=0, keepdims=True)
         mt[it, :, LANES : 2 * LANES] = pack(sq_p, sq_d)
-        nb_src[1 + r] = ys[0, 0:1, :]
+        nb_src[1 + r] = ys[0:1, :]
         tm_send(it)
         to_next(1 + r, r, -1)
 
@@ -494,7 +497,7 @@
         to_next(4 + r, r, 1)
 
         next_wait(1 + r)
-        following = pltpu.roll(ys[0], hours - 1, 0)
+        following = pltpu.roll(ys[rows_of(0), :], hours - 1, 0)
         following = jnp.where(row == hours - 1, nb_dst[1 + r] * has_after, following)
         grad[0] = grad[0] + following
 
@@ -525,7 +528,7 @@
             recv_g.at[it],
         )
         next_wait(4 + r)
-        prev_grad = nb_dst[4 + r] + ys[0, 0:1, :]
+        prev_grad = nb_dst[4 + r] + ys[0:1, :]
 
         pltpu.make_async_copy(sbuf.at[r], sbuf.at[r], recv_r.at[r]).wait()
         sums = mr[r]
@@ -544,7 +547,7 @@
         dual_step = STEP_SCALE * weight
 
         def primal(c, a):
-            bar, sq = primal_block(c, xs[c], grad[c], primal_step)
+            bar, sq = primal_block(c, xs[rows_of(c), :], grad[c], primal_step)
             return bar, a + fold(sq)
 
         bar0, sq_p = primal(0, zero8)
@@ -593,15 +596,16 @@
         pltpu.make_async_copy(nb_src.at[n], nb_src.at[n], send_n.at[n]).wait()
 
 
-def by_hour(x, y, cap, own):
-    cb, hours, _, bs = x.shape
+def to_results(x, y, cap, own):
+    rows = x.shape[0]
+    pieces = 4
 
     def place(x_ref, y_ref, cap_ref, x_out, y_out, cap_out, sem):
         copies = []
-        for c in range(cb):
-            at = pl.ds(c * bs, bs)
-            copies.append(pltpu.make_async_copy(x_ref.at[c], x_out.at[:, :, at], sem.at[0, c]))
-            copies.append(pltpu.make_async_copy(y_ref.at[c], y_out.at[:, :, at], sem.at[1, c]))
+        for n in range(pieces):
+            at = pl.ds(n * (rows // pieces), rows // pieces)
+            copies.append(pltpu.make_async_copy(x_ref.at[at], x_out.at[at], sem.at[0, n]))
+            copies.append(pltpu.make_async_copy(y_ref.at[at], y_out.at[at], sem.at[1, n]))
         for copy in copies:
             copy.start()
         cap_out[...] = cap_ref[:, 0:own]
@@ -610,13 +614,13 @@
 
     vmem = pl.BlockSpec(memory_space=pltpu.VMEM)
     hbm = pl.BlockSpec(memory_space=pl.ANY)
-    shape = jax.ShapeDtypeStruct((hours, 1, cb * bs), F32)
+    shape = jax.ShapeDtypeStruct(x.shape, F32)
     return pl.pallas_call(
         place,
         in_specs=[vmem, vmem, vmem],
         out_specs=(hbm, hbm, vmem),
         out_shape=(shape, shape, jax.ShapeDtypeStruct((1, own), F32)),
-        scratch_shapes=[pltpu.SemaphoreType.DMA((2, cb))],
+        scratch_shapes=[pltpu.SemaphoreType.DMA((2, pieces))],
         compiler_params=pltpu.CompilerParams(vmem_limit_bytes=8 * 2**20),
     )(x, y, cap)
 
@@ -653,8 +657,8 @@
     x_new, y_new, cap = pl.pallas_call(
         functools.partial(kernel, sizes),
         out_shape=(
-            jax.ShapeDtypeStruct((cb, hours, bs), F32),
-            jax.ShapeDtypeStruct((cb, hours, bs), F32),
+            jax.ShapeDtypeStruct((hours * cb, bs), F32),
+            jax.ShapeDtypeStruct((hours * cb, bs), F32),
             jax.ShapeDtypeStruct((1, LANES), F32),
         ),
         in_specs=[hbm] * 10,
@@ -698,7 +702,7 @@
             pltpu.VMEM((1 + 2 * rounds, 1, LANES), F32),
             pltpu.VMEM((1 + 2 * rounds, 1, LANES), F32),
             dma((11,)),
-            dma((cb,)),
+            dma((cb // 5 if cb % 5 == 0 else cb,)),
             dma((ITERS,)),
             dma((ITERS,)),
             dma((rounds,)),
@@ -725,8 +729,8 @@
         net_weights[0],
         line_weights.reshape(nl * bs, bs),
     )))
-    parts = (cb, hours, 1, bs)
-    return by_hour(x_new.reshape(parts), y_new.reshape(parts), cap, start_capacity.shape[1])
+    x_new, y_new, capacity = to_results(x_new, y_new, cap, start_capacity.shape[1])
+    return x_new.reshape(hours, 1, width), y_new.reshape(hours, 1, width), capacity
 
 
 def solution(mesh):

time: 55.9 us -> 55.3 us (0.989)
  no operation moved by 1% of the time
where the time goes in v6:
time: 55.3 us; the launch traced here: 55.2 us
  Pallas kernels  54.6 us (99%)
  between operations  0.64 us (1%)
    pallas_call x1, Pallas kernels, body(): pl.pallas_call(functools.partial(kernel, sizes), out_shape=(jax.ShapeDtyp...  52.8 us
    pallas_call x1, Pallas kernels, to_results(): pl.pallas_call(place, in_specs=[vmem, vmem, vmem], out_specs=(hbm, hbm, v...  1.73 us

profile of v6, /device:TPU:1, one launch (start us, length us, event | category | flops | bytes accessed | tf_op | source)
XLA Modules:
  0.0 55.2 jit_solution(5015862075320558165)
XLA Ops:
  0.6 52.8 %shard_map.121 = (f32[1600,128]{1,0:T(8,128)S(1)}, f32[1600,128]{1,0:T(8,128)S(1)}, f32[1,128]{1,0:T(1,128)S(1)}) custom-call(s32[3,1,25]{2,1,0:T(1,128)} %bitcast.15, s32[4,8]{1,0:T(4,128)} %bitcast.14, f32[1,4]{1,0:T(1,128)} %cap_hbm.1, f32[1,4]{1,0:T(1,128)} %build_hbm.1, s32[1,128]{1,0:T(1,128)} %gm_hbm.1, f32[25,1,128]{2,1,0:T(1,128)} %bitcast.13, ...), custom_call_target="tpu_custom_call" | custom-call | tf_op jit(solution)/shard_map/pallas_call | solution.py:657
  53.5 1.7 %shard_map.122 = (f32[1600,128]{1,0:T(8,128)}, f32[1600,128]{1,0:T(8,128)}, f32[1,4]{1,0:T(1,128)}) custom-call(f32[1600,128]{1,0:T(8,128)S(1)} %get-tuple-element.9.x_ref, f32[1600,128]{1,0:T(8,128)S(1)} %get-tuple-element.10.y_ref, f32[1,128]{1,0:T(1,128)S(1)} %get-tuple-element.11.cap_ref), custom_call_target="tpu_custom_call" | custom-call | tf_op jit(solution)/shard_map/pallas_call | solution.py:618

commit v7 on v6

--- a/solution.py
+++ b/solution.py
@@ -208,12 +208,14 @@
 
         tm_partners(send)
 
-    def tm_sum(r):
-        pltpu.make_async_copy(tbuf.at[r], tbuf.at[r], recv_t.at[r]).wait()
-        parts = [mt[r]] + [tbuf[r, k] for k in range(nt - 1)]
+    def tree(parts):
         while len(parts) > 1:
             parts = [sum(parts[n + 1 : n + 2], parts[n]) for n in range(0, len(parts), 2)]
         return parts[0]
+
+    def tm_sum(r):
+        pltpu.make_async_copy(tbuf.at[r], tbuf.at[r], recv_t.at[r]).wait()
+        return tree([mt[r]] + [tbuf[r, k] for k in range(nt - 1)])
 
     def region_send(src, dst_of, send_sem, recv_sem):
         @pl.loop(0, nr - 1)
@@ -408,16 +410,14 @@
         if first:
             picked = capacity_term()
         sq = sq + dual_block(2, rest - picked, step, first)
-        return sq + dual_block(1, last - line_flow(), step, first)
+        cols = jnp.sum(ys[rows_of(2), :], axis=0, keepdims=True)
+        return sq + dual_block(1, last - line_flow(), step, first), cols
 
     lane_low = lane < LANES // 2
 
-    def pack(p, d):
-        p = jnp.sum(p, axis=0, keepdims=True)
-        d = jnp.sum(d, axis=0, keepdims=True)
-        p = p + pltpu.roll(p, LANES // 2, 1)
-        d = d + pltpu.roll(d, LANES // 2, 1)
-        return jnp.where(lane_low, p, d)
+    def halves(v):
+        v = jnp.sum(v, axis=0, keepdims=True)
+        return v + pltpu.roll(v, LANES // 2, 1)
 
     gathered = []
 
@@ -445,16 +445,17 @@
     prev_old = nb_dst[0]
     prev_new = jnp.maximum(prev_old - first_step * unit_v[0], 0.0)
     prev_bar = prev_new + (prev_new - prev_old)
-    sq_d = forward(bar0, prev_bar, first_capacity, first_flow, first_step, True)
+    sq_p = halves(sq_p)
+    sq_d, col_own = forward(bar0, prev_bar, first_capacity, first_flow, first_step, True)
     cap_old, build, cap_new = gathered
 
     c2.wait()
 
     def later(it, carry):
-        prev_x, cap, cap_change, weight, sq_p, sq_d = carry
+        prev_x, cap, cap_change, weight, sq_p, sq_d, col_own = carry
         r = it - 1
-        mt[it, :, 0:LANES] = jnp.sum(ys[rows_of(2), :], axis=0, keepdims=True)
-        mt[it, :, LANES : 2 * LANES] = pack(sq_p, sq_d)
+        mt[it, :, 0:LANES] = col_own
+        mt[it, :, LANES : 2 * LANES] = jnp.where(lane_low, sq_p, halves(sq_d))
         nb_src[1 + r] = ys[0:1, :]
         tm_send(it)
         to_next(1 + r, r, -1)
@@ -503,9 +504,7 @@
 
         total = tm_sum(it)
         col_sums = total[:, 0:LANES]
-        region_sums = total[:, LANES : 2 * LANES] + pack(
-            cap_change, jnp.zeros_like(cap_change)
-        )
+        region_sums = total[:, LANES : 2 * LANES] + cap_change
         mr[r] = region_sums
         region_send(
             lambda k: mr.at[r], lambda k: sbuf.at[r, k - 1], send_r.at[r], recv_r.at[r]
@@ -531,9 +530,7 @@
         prev_grad = nb_dst[4 + r] + ys[0:1, :]
 
         pltpu.make_async_copy(sbuf.at[r], sbuf.at[r], recv_r.at[r]).wait()
-        sums = mr[r]
-        for k in range(nr - 1):
-            sums = sums + sbuf[r, k]
+        sums = tree([mr[r]] + [sbuf[r, k] for k in range(nr - 1)])
         total_p = jnp.sum(jnp.where(lane_low, sums, 0.0), axis=1, keepdims=True)
         total_d = jnp.sum(jnp.where(lane_low, 0.0, sums), axis=1, keepdims=True)
         total_p = jnp.broadcast_to(total_p, (1, LANES))
@@ -551,7 +548,7 @@
             return bar, a + fold(sq)
 
         bar0, sq_p = primal(0, zero8)
-        sq_p = unrolled(1, cb, 6, lambda c, a: primal(c, a)[1], sq_p)
+        sq_p = unrolled(1, cb, 12, lambda c, a: primal(c, a)[1], sq_p)
         new_cap = jnp.maximum(cap - primal_step * (build - capacity_grad), 0.0)
         cap_diff = new_cap - cap
         prev_new = jnp.maximum(prev_x - primal_step * prev_grad, 0.0)
@@ -566,17 +563,20 @@
             line_a[...] = new_line
             return new_line - primal_step * line_grad
 
-        sq_d = forward(bar0, prev_bar, lambda: new_cap + cap_diff, flow, dual_step, False)
-        return prev_new, new_cap, cap_diff * cap_diff, weight, sq_p, sq_d
+        sq_p = halves(sq_p)
+        cap_change = jnp.where(lane_low, halves(cap_diff * cap_diff), 0.0)
+        sq_d, col_own = forward(bar0, prev_bar, lambda: new_cap + cap_diff, flow, dual_step, False)
+        return prev_new, new_cap, cap_change, weight, sq_p, sq_d, col_own
 
     first_diff = cap_new - cap_old
     carry = (
         prev_new,
         cap_new,
-        first_diff * first_diff,
+        jnp.where(lane_low, halves(first_diff * first_diff), 0.0),
         jnp.ones((1, LANES), F32),
         sq_p,
         sq_d,
+        col_own,
     )
     carry = lax.fori_loop(1, ITERS, later, carry)
     cap_out[...] = pltpu.roll(carry[1], lax.rem(LANES - me_t * own_n, LANES), 1)

time: 55.3 us -> 55.2 us (level)
  no operation moved by 1% of the time
where the time goes in v7:
time: 55.2 us; the launch traced here: 55.1 us
  Pallas kernels  54.5 us (99%)
  between operations  0.64 us (1%)
    pallas_call x1, Pallas kernels, body(): pl.pallas_call(functools.partial(kernel, sizes), out_shape=(jax.ShapeDtyp...  52.7 us
    pallas_call x1, Pallas kernels, to_results(): pl.pallas_call(place, in_specs=[vmem, vmem, vmem], out_specs=(hbm, hbm, v...  1.73 us

profile of v7, /device:TPU:1, one launch (start us, length us, event | category | flops | bytes accessed | tf_op | source)
XLA Modules:
  0.0 55.1 jit_solution(12251613380004594014)
XLA Ops:
  0.6 52.7 %shard_map.121 = (f32[1600,128]{1,0:T(8,128)S(1)}, f32[1600,128]{1,0:T(8,128)S(1)}, f32[1,128]{1,0:T(1,128)S(1)}) custom-call(s32[3,1,25]{2,1,0:T(1,128)} %bitcast.15, s32[4,8]{1,0:T(4,128)} %bitcast.14, f32[1,4]{1,0:T(1,128)} %cap_hbm.1, f32[1,4]{1,0:T(1,128)} %build_hbm.1, s32[1,128]{1,0:T(1,128)} %gm_hbm.1, f32[25,1,128]{2,1,0:T(1,128)} %bitcast.13, ...), custom_call_target="tpu_custom_call" | custom-call | tf_op jit(solution)/shard_map/pallas_call | solution.py:657
  53.4 1.7 %shard_map.122 = (f32[1600,128]{1,0:T(8,128)}, f32[1600,128]{1,0:T(8,128)}, f32[1,4]{1,0:T(1,128)}) custom-call(f32[1600,128]{1,0:T(8,128)S(1)} %get-tuple-element.9.x_ref, f32[1600,128]{1,0:T(8,128)S(1)} %get-tuple-element.10.y_ref, f32[1,128]{1,0:T(1,128)S(1)} %get-tuple-element.11.cap_ref), custom_call_target="tpu_custom_call" | custom-call | tf_op jit(solution)/shard_map/pallas_call | solution.py:618
